TPU v7x, 256 devices: a whole 4x4x8 slice. The times are simulated.
256 devices in a mesh: gx: 8 (over z_hi, core), gy: 8 (over z_lo, y), gz: 4 (over x).
Axes of the slice: x: 4, y: 4, z: 8 (z_hi: 4, z_lo: 2; z = z_hi * 2 + z_lo), core: 2. Of those that a mesh axis runs over, the one named last changes fastest.
Arguments:
- blocks: bfloat16 [16, 8, 8, 27, 128, 128], P('gx', 'gy', 'gz')
- pattern: int32 [16, 8, 8, 27], P('gx', 'gy'), may hold values 0 or 1
- order: int32 [16, 8, 8], P('gx', 'gy'), may hold values from 0 to 7, each once within a row
- start: float32 [16, 8, 8, 128], P('gx', 'gy', 'gz'), may hold values from -6 to 6
- rhs: float32 [16, 8, 8, 128], P('gx', 'gy', 'gz'), may hold values from -6 to 6
Outputs:
- smoothed: float32 [16, 8, 8, 128], P('gx', 'gy', 'gz')
- remainder: float32 [16, 8, 8, 128], P('gx', 'gy', 'gz')
Inputs may be any that keep to these rules, and one draw needn't show every extreme that they name: `order`: in every grid column the 8 slots name each plane exactly once. `pattern`: entry 13 is ignored.
All inputs are finite; a program needn't handle non-finite values. No bound on the sum of `pattern` on one device may be relied on, other than what follows from the above.
Results may differ from a plain program's by a relative error of at most 0.0081.
Values may be sent and summed in bfloat16 or wider, within the bound.
A program may use at most 64 MiB of HBM per device.

v0:
```python
import jax
import jax.numpy as jnp
from jax import lax
from jax.sharding import PartitionSpec as P

DEG = 4


def padded_2(cells, sides, width):
    for axis, dim in sides:
        count = lax.axis_size(axis)
        ends = count - 1
        head = lax.slice_in_dim(cells, 0, width, axis=dim)
        tail = lax.slice_in_dim(cells, cells.shape[dim] - width, cells.shape[dim], axis=dim)
        cells = jnp.concatenate(
            [
                lax.ppermute(tail, axis, [(i, (i + 1) % count) for i in range(ends)]),
                cells,
                lax.ppermute(head, axis, [((i + 1) % count, i) for i in range(ends)]),
            ],
            axis=dim,
        )
    return cells


def coupled_product(matrix, planes, rows, present):
    padded = padded_2(planes, (("gx", 0), ("gy", 1)), 1)
    padded = jnp.pad(padded, ((0, 0), (0, 0), (1, 1), (0, 0)))
    span_x, span_y = (planes.shape[0], planes.shape[1])
    height = padded.shape[2]
    keeping = jnp.where(jnp.arange(27) == 13, 1, present).astype(jnp.float32)
    offsets = jnp.arange(3, dtype=jnp.int32)
    places = jnp.arange(height, dtype=jnp.int32)
    target = rows[..., None, None] + offsets[:, None]
    select = (target == places).astype(jnp.float32)
    pieces = []
    for step_a in range(3):
        for step_b in range(3):
            column = padded[step_a : step_a + span_x, step_b : step_b + span_y]
            first = 9 * step_a + 3 * step_b
            table = (select * keeping[..., first : first + 3, None]).astype(jnp.bfloat16)
            picked = jnp.einsum(
                "xyscp,xypw->xyscw", table, column, preferred_element_type=jnp.float32
            )
            pieces.append(picked.astype(jnp.bfloat16))
    gathered = jnp.stack(pieces, axis=3)
    gathered = gathered.reshape(gathered.shape[:3] + (27, gathered.shape[-1]))
    return jnp.einsum("xysoj,xysoij->xysi", gathered, matrix, preferred_element_type=jnp.float32)


def by_plane(vector, order):
    places = jnp.arange(order.shape[2], dtype=jnp.int32)
    table = (order[..., None] == places).astype(jnp.bfloat16)
    moved = jnp.einsum("xysp,xysw->xypw", table, vector, preferred_element_type=jnp.float32)
    return moved.astype(jnp.bfloat16)


def local(blocks, pattern, order, start, rhs):
    depth = blocks.shape[2]
    first = lax.axis_index("gz") * depth
    smoothed, target = (start, rhs)
    rows = lax.dynamic_slice_in_dim(order, first, depth, 2)
    present = lax.dynamic_slice_in_dim(pattern, first, depth, 2)

    def operator(vector):
        column = lax.all_gather(vector.astype(jnp.bfloat16), "gz", axis=2, tiled=True)
        planes = by_plane(column, order)
        return coupled_product(blocks, planes, rows, present)

    center = 1.0
    spread = 0.8
    sigma = center / spread
    rho = 1.0 / sigma
    remainder = target - operator(smoothed)
    search = remainder / center
    for number in range(DEG):
        smoothed = smoothed + search
        remainder = remainder - operator(search)
        if number + 1 < DEG:
            following = 1.0 / (2.0 * sigma - rho)
            search = following * rho * search + 2.0 * following / spread * remainder
            rho = following
    return (smoothed, remainder)


def solution(mesh):
    in_specs = (
        P("gx", "gy", "gz", None, None, None),
        P("gx", "gy", None, None),
        P("gx", "gy", None),
        P("gx", "gy", "gz", None),
        P("gx", "gy", "gz", None),
    )
    out_specs = (P("gx", "gy", "gz", None), P("gx", "gy", "gz", None))
    return jax.shard_map(local, mesh=mesh, in_specs=in_specs, out_specs=out_specs, check_vma=False)
```

profile of v0, /device:TPU:97, one launch (start us, length us, event | category | flops | bytes accessed | tf_op | source)
XLA Modules:
  0.0 160.3 jit_solution(5242034563477572541)
XLA Ops:
  0.7 0.8 copy.155
  1.5 7.8 %all_gather.15 = bf16[2,1,8,128]{3,0,1,2:T(2,128)(2,1)S(1)} all-gather(bf16[2,1,2,128]{3,0,1,2:T(2,128)(2,1)S(1)} %copy.155), channel_id=1, replica_groups=mesh['gx'=8,'gy'=8,'gz'=4] {'gz'}, dimensions={2}, use_global_device_ids=true | all-gather | bytes 5120 | tf_op jit(solution)/shard_map/all_gather | solution.py:66
  9.3 0.8 convolution_convert_fusion.49
  10.1 0.6 slice_bitcast_fusion.107
  10.7 7.8 %collective-permute-start = (bf16[1,1,8,128]{3,2,0,1:T(8,128)(2,1)}, bf16[1,1,8,128]{3,2,0,1:T(8,128)(2,1)S(1)}, u32[]{:S(2)}, u32[]{:S(2)}) collective-permute-start(bf16[1,1,8,128]{3,2,0,1:T(8,128)(2,1)} %get-tuple-element.24), channel_id=1, source_target_pairs={{0,32},{32,64},{64,96},{96,128},{128,160},{160,192},{192,224},{1,3... | collective-permute-start | bytes 6152 | tf_op jit(solution)/shard_map/ppermute | solution.py:17
  18.5 1.9 %collective-permute-start.1 = (bf16[1,1,8,128]{3,2,1,0:T(8,128)(2,1)}, bf16[1,1,8,128]{3,2,1,0:T(8,128)(2,1)S(1)}, u32[]{:S(2)}, u32[]{:S(2)}) collective-permute-start(bf16[1,1,8,128]{3,2,1,0:T(8,128)(2,1)} %get-tuple-element.25), channel_id=1, source_target_pairs={{32,0},{64,32},{96,64},{128,96},{160,128},{192,160},{224,192},{33,... | collective-permute-start | bytes 6152 | tf_op jit(solution)/shard_map/ppermute | solution.py:19
  20.4 0.6 iota_compare_fusion.9
  21.0 0.7 select_convert_fusion.54
  21.8 0.8 constant_dynamic-slice_fusion
  22.6 3.1 %collective-permute-done.1 = bf16[1,1,8,128]{3,2,1,0:T(8,128)(2,1)S(1)} collective-permute-done((bf16[1,1,8,128]{3,2,1,0:T(8,128)(2,1)}, bf16[1,1,8,128]{3,2,1,0:T(8,128)(2,1)S(1)}, u32[]{:S(2)}, u32[]{:S(2)}) %collective-permute-start.1) | collective-permute-done | bytes 2080 | tf_op jit(solution)/shard_map/ppermute | solution.py:19
  25.7 5.1 %collective-permute-start.3 = (bf16[4,1,8,128]{3,2,0,1:T(8,128)(2,1)S(1)}, bf16[4,1,8,128]{3,2,0,1:T(8,128)(2,1)S(1)}, u32[]{:S(2)}, u32[]{:S(2)}) collective-permute-start(bf16[4,1,8,128]{3,2,0,1:T(8,128)(2,1)S(1)} %pad_maximum_fusion), channel_id=1, source_target_pairs={{4,0},{8,4},{12,8},{16,12},{20,16},{24,20},{28,24},{5,1},{9,5},{13... | collective-permute-start | bytes 24584 | tf_op jit(solution)/shard_map/ppermute | solution.py:19
  30.8 1.9 %collective-permute-start.2 = (bf16[4,1,8,128]{3,2,0,1:T(8,128)(2,1)S(1)}, bf16[4,1,8,128]{3,2,0,1:T(8,128)(2,1)S(1)}, u32[]{:S(2)}, u32[]{:S(2)}) collective-permute-start(bf16[4,1,8,128]{3,2,0,1:T(8,128)(2,1)S(1)} %pad_maximum_fusion), channel_id=1, source_target_pairs={{0,4},{4,8},{8,12},{12,16},{16,20},{20,24},{24,28},{1,5},{5,9},{9,... | collective-permute-start | bytes 24584 | tf_op jit(solution)/shard_map/ppermute | solution.py:17
  32.8 4.5 %collective-permute-done.2 = bf16[4,1,8,128]{3,2,0,1:T(8,128)(2,1)S(1)} collective-permute-done((bf16[4,1,8,128]{3,2,0,1:T(8,128)(2,1)S(1)}, bf16[4,1,8,128]{3,2,0,1:T(8,128)(2,1)S(1)}, u32[]{:S(2)}, u32[]{:S(2)}) %collective-permute-start.2) | collective-permute-done | bytes 8224 | tf_op jit(solution)/shard_map/ppermute | solution.py:17
  38.4 0.2 fusion.21
  38.6 0.2 fusion.23
  38.8 0.2 fusion.25
  39.0 0.2 fusion.27
  39.2 1.0 fusion.8
  40.3 5.3 %all_gather.16 = bf16[2,1,8,128]{3,0,1,2:T(2,128)(2,1)S(1)} all-gather(bf16[2,1,2,128]{3,0,1,2:T(2,128)(2,1)S(1)} %get-tuple-element.12), channel_id=1, replica_groups=mesh['gx'=8,'gy'=8,'gz'=4] {'gz'}, dimensions={2}, use_global_device_ids=true | all-gather | bytes 5120 | tf_op jit(solution)/shard_map/all_gather | solution.py:66
  45.7 5.8 %collective-permute-start.4 = (bf16[1,1,8,128]{3,2,0,1:T(8,128)(2,1)S(1)}, bf16[1,1,8,128]{3,2,0,1:T(8,128)(2,1)S(1)}, u32[]{:S(2)}, u32[]{:S(2)}) collective-permute-start(bf16[1,1,8,128]{3,2,0,1:T(8,128)(2,1)S(1)} %get-tuple-element.22), channel_id=1, source_target_pairs={{0,32},{32,64},{64,96},{96,128},{128,160},{160,192},{192,224},{1,3... | collective-permute-start | bytes 6152 | tf_op jit(solution)/shard_map/ppermute | solution.py:17
  51.4 1.9 %collective-permute-start.5 = (bf16[1,1,8,128]{3,2,1,0:T(8,128)(2,1)S(1)}, bf16[1,1,8,128]{3,2,1,0:T(8,128)(2,1)S(1)}, u32[]{:S(2)}, u32[]{:S(2)}) collective-permute-start(bf16[1,1,8,128]{3,2,1,0:T(8,128)(2,1)S(1)} %get-tuple-element.23), channel_id=1, source_target_pairs={{32,0},{64,32},{96,64},{128,96},{160,128},{192,160},{224,192},{33,... | collective-permute-start | bytes 6152 | tf_op jit(solution)/shard_map/ppermute | solution.py:19
  53.4 5.1 %collective-permute-done.5 = bf16[1,1,8,128]{3,2,1,0:T(8,128)(2,1)S(1)} collective-permute-done((bf16[1,1,8,128]{3,2,1,0:T(8,128)(2,1)S(1)}, bf16[1,1,8,128]{3,2,1,0:T(8,128)(2,1)S(1)}, u32[]{:S(2)}, u32[]{:S(2)}) %collective-permute-start.5) | collective-permute-done | bytes 2080 | tf_op jit(solution)/shard_map/ppermute | solution.py:19
  58.5 1.9 %collective-permute-start.7 = (bf16[4,1,8,128]{3,2,0,1:T(8,128)(2,1)S(1)}, bf16[4,1,8,128]{3,2,0,1:T(8,128)(2,1)S(1)}, u32[]{:S(2)}, u32[]{:S(2)}) collective-permute-start(bf16[4,1,8,128]{3,2,0,1:T(8,128)(2,1)S(1)} %pad_maximum_fusion.1), channel_id=1, source_target_pairs={{4,0},{8,4},{12,8},{16,12},{20,16},{24,20},{28,24},{5,1},{9,5},{13... | collective-permute-start | bytes 24584 | tf_op jit(solution)/shard_map/ppermute | solution.py:19
  60.4 3.4 %collective-permute-start.6 = (bf16[4,1,8,128]{3,2,0,1:T(8,128)(2,1)S(1)}, bf16[4,1,8,128]{3,2,0,1:T(8,128)(2,1)S(1)}, u32[]{:S(2)}, u32[]{:S(2)}) collective-permute-start(bf16[4,1,8,128]{3,2,0,1:T(8,128)(2,1)S(1)} %pad_maximum_fusion.1), channel_id=1, source_target_pairs={{0,4},{4,8},{8,12},{12,16},{16,20},{20,24},{24,28},{1,5},{5,9},{9,... | collective-permute-start | bytes 24584 | tf_op jit(solution)/shard_map/ppermute | solution.py:17
  63.8 3.1 %collective-permute-done.6 = bf16[4,1,8,128]{3,2,0,1:T(8,128)(2,1)S(1)} collective-permute-done((bf16[4,1,8,128]{3,2,0,1:T(8,128)(2,1)S(1)}, bf16[4,1,8,128]{3,2,0,1:T(8,128)(2,1)S(1)}, u32[]{:S(2)}, u32[]{:S(2)}) %collective-permute-start.6) | collective-permute-done | bytes 8224 | tf_op jit(solution)/shard_map/ppermute | solution.py:17
  67.9 0.2 fusion.39
  68.3 0.2 fusion.43
  68.5 0.2 fusion.45
  68.8 1.0 fusion.6
  69.8 7.0 %all_gather.17 = bf16[2,1,8,128]{3,0,1,2:T(2,128)(2,1)S(1)} all-gather(bf16[2,1,2,128]{3,0,1,2:T(2,128)(2,1)S(1)} %get-tuple-element.10), channel_id=1, replica_groups=mesh['gx'=8,'gy'=8,'gz'=4] {'gz'}, dimensions={2}, use_global_device_ids=true | all-gather | bytes 5120 | tf_op jit(solution)/shard_map/all_gather | solution.py:66
  76.9 5.1 %collective-permute-start.8 = (bf16[1,1,8,128]{3,2,0,1:T(8,128)(2,1)S(1)}, bf16[1,1,8,128]{3,2,0,1:T(8,128)(2,1)S(1)}, u32[]{:S(2)}, u32[]{:S(2)}) collective-permute-start(bf16[1,1,8,128]{3,2,0,1:T(8,128)(2,1)S(1)} %get-tuple-element.20), channel_id=1, source_target_pairs={{0,32},{32,64},{64,96},{96,128},{128,160},{160,192},{192,224},{1,3... | collective-permute-start | bytes 6152 | tf_op jit(solution)/shard_map/ppermute | solution.py:17
  82.1 1.9 %collective-permute-start.9 = (bf16[1,1,8,128]{3,2,1,0:T(8,128)(2,1)S(1)}, bf16[1,1,8,128]{3,2,1,0:T(8,128)(2,1)S(1)}, u32[]{:S(2)}, u32[]{:S(2)}) collective-permute-start(bf16[1,1,8,128]{3,2,1,0:T(8,128)(2,1)S(1)} %get-tuple-element.21), channel_id=1, source_target_pairs={{32,0},{64,32},{96,64},{128,96},{160,128},{192,160},{224,192},{33,... | collective-permute-start | bytes 6152 | tf_op jit(solution)/shard_map/ppermute | solution.py:19
  84.0 5.1 %collective-permute-done.9 = bf16[1,1,8,128]{3,2,1,0:T(8,128)(2,1)S(1)} collective-permute-done((bf16[1,1,8,128]{3,2,1,0:T(8,128)(2,1)S(1)}, bf16[1,1,8,128]{3,2,1,0:T(8,128)(2,1)S(1)}, u32[]{:S(2)}, u32[]{:S(2)}) %collective-permute-start.9) | collective-permute-done | bytes 2080 | tf_op jit(solution)/shard_map/ppermute | solution.py:19
  89.1 1.9 %collective-permute-start.11 = (bf16[4,1,8,128]{3,2,0,1:T(8,128)(2,1)S(1)}, bf16[4,1,8,128]{3,2,0,1:T(8,128)(2,1)S(1)}, u32[]{:S(2)}, u32[]{:S(2)}) collective-permute-start(bf16[4,1,8,128]{3,2,0,1:T(8,128)(2,1)S(1)} %pad_maximum_fusion.2), channel_id=1, source_target_pairs={{4,0},{8,4},{12,8},{16,12},{20,16},{24,20},{28,24},{5,1},{9,5},{13... | collective-permute-start | bytes 24584 | tf_op jit(solution)/shard_map/ppermute | solution.py:19
  91.0 3.4 %collective-permute-start.10 = (bf16[4,1,8,128]{3,2,0,1:T(8,128)(2,1)S(1)}, bf16[4,1,8,128]{3,2,0,1:T(8,128)(2,1)S(1)}, u32[]{:S(2)}, u32[]{:S(2)}) collective-permute-start(bf16[4,1,8,128]{3,2,0,1:T(8,128)(2,1)S(1)} %pad_maximum_fusion.2), channel_id=1, source_target_pairs={{0,4},{4,8},{8,12},{12,16},{16,20},{20,24},{24,28},{1,5},{5,9},{9,... | collective-permute-start | bytes 24584 | tf_op jit(solution)/shard_map/ppermute | solution.py:17
  94.4 3.1 %collective-permute-done.10 = bf16[4,1,8,128]{3,2,0,1:T(8,128)(2,1)S(1)} collective-permute-done((bf16[4,1,8,128]{3,2,0,1:T(8,128)(2,1)S(1)}, bf16[4,1,8,128]{3,2,0,1:T(8,128)(2,1)S(1)}, u32[]{:S(2)}, u32[]{:S(2)}) %collective-permute-start.10) | collective-permute-done | bytes 8224 | tf_op jit(solution)/shard_map/ppermute | solution.py:17
  98.5 0.2 fusion.57
  98.9 0.2 fusion.61
  99.1 0.2 fusion.63
  99.4 1.0 fusion.4
  100.5 5.3 %all_gather.18 = bf16[2,1,8,128]{3,0,1,2:T(2,128)(2,1)S(1)} all-gather(bf16[2,1,2,128]{3,0,1,2:T(2,128)(2,1)S(1)} %get-tuple-element.8), channel_id=1, replica_groups=mesh['gx'=8,'gy'=8,'gz'=4] {'gz'}, dimensions={2}, use_global_device_ids=true | all-gather | bytes 5120 | tf_op jit(solution)/shard_map/all_gather | solution.py:66
  105.8 4.8 %collective-permute-start.12 = (bf16[1,1,8,128]{3,2,0,1:T(8,128)(2,1)S(1)}, bf16[1,1,8,128]{3,2,0,1:T(8,128)(2,1)S(1)}, u32[]{:S(2)}, u32[]{:S(2)}) collective-permute-start(bf16[1,1,8,128]{3,2,0,1:T(8,128)(2,1)S(1)} %get-tuple-element.18), channel_id=1, source_target_pairs={{0,32},{32,64},{64,96},{96,128},{128,160},{160,192},{192,224},{1,3... | collective-permute-start | bytes 6152 | tf_op jit(solution)/shard_map/ppermute | solution.py:17
  110.7 1.9 %collective-permute-start.13 = (bf16[1,1,8,128]{3,2,1,0:T(8,128)(2,1)S(1)}, bf16[1,1,8,128]{3,2,1,0:T(8,128)(2,1)S(1)}, u32[]{:S(2)}, u32[]{:S(2)}) collective-permute-start(bf16[1,1,8,128]{3,2,1,0:T(8,128)(2,1)S(1)} %get-tuple-element.19), channel_id=1, source_target_pairs={{32,0},{64,32},{96,64},{128,96},{160,128},{192,160},{224,192},{33,... | collective-permute-start | bytes 6152 | tf_op jit(solution)/shard_map/ppermute | solution.py:19
  112.6 5.1 %collective-permute-done.13 = bf16[1,1,8,128]{3,2,1,0:T(8,128)(2,1)S(1)} collective-permute-done((bf16[1,1,8,128]{3,2,1,0:T(8,128)(2,1)S(1)}, bf16[1,1,8,128]{3,2,1,0:T(8,128)(2,1)S(1)}, u32[]{:S(2)}, u32[]{:S(2)}) %collective-permute-start.13) | collective-permute-done | bytes 2080 | tf_op jit(solution)/shard_map/ppermute | solution.py:19
  117.7 1.9 %collective-permute-start.15 = (bf16[4,1,8,128]{3,2,0,1:T(8,128)(2,1)S(1)}, bf16[4,1,8,128]{3,2,0,1:T(8,128)(2,1)S(1)}, u32[]{:S(2)}, u32[]{:S(2)}) collective-permute-start(bf16[4,1,8,128]{3,2,0,1:T(8,128)(2,1)S(1)} %pad_maximum_fusion.3), channel_id=1, source_target_pairs={{4,0},{8,4},{12,8},{16,12},{20,16},{24,20},{28,24},{5,1},{9,5},{13... | collective-permute-start | bytes 24584 | tf_op jit(solution)/shard_map/ppermute | solution.py:19
  119.6 3.4 %collective-permute-start.14 = (bf16[4,1,8,128]{3,2,0,1:T(8,128)(2,1)S(1)}, bf16[4,1,8,128]{3,2,0,1:T(8,128)(2,1)S(1)}, u32[]{:S(2)}, u32[]{:S(2)}) collective-permute-start(bf16[4,1,8,128]{3,2,0,1:T(8,128)(2,1)S(1)} %pad_maximum_fusion.3), channel_id=1, source_target_pairs={{0,4},{4,8},{8,12},{12,16},{16,20},{20,24},{24,28},{1,5},{5,9},{9,... | collective-permute-start | bytes 24584 | tf_op jit(solution)/shard_map/ppermute | solution.py:17
  123.0 3.1 %collective-permute-done.14 = bf16[4,1,8,128]{3,2,0,1:T(8,128)(2,1)S(1)} collective-permute-done((bf16[4,1,8,128]{3,2,0,1:T(8,128)(2,1)S(1)}, bf16[4,1,8,128]{3,2,0,1:T(8,128)(2,1)S(1)}, u32[]{:S(2)}, u32[]{:S(2)}) %collective-permute-start.14) | collective-permute-done | bytes 8224 | tf_op jit(solution)/shard_map/ppermute | solution.py:17
  127.2 0.2 fusion.75
  127.6 0.2 fusion.79
  127.8 0.2 fusion.81
  128.0 1.0 fusion.2
  129.1 7.0 %all_gather.19 = bf16[2,1,8,128]{3,0,1,2:T(2,128)(2,1)S(1)} all-gather(bf16[2,1,2,128]{3,0,1,2:T(2,128)(2,1)S(1)} %get-tuple-element.14), channel_id=1, replica_groups=mesh['gx'=8,'gy'=8,'gz'=4] {'gz'}, dimensions={2}, use_global_device_ids=true | all-gather | bytes 5120 | tf_op jit(solution)/shard_map/all_gather | solution.py:66
  136.2 5.1 %collective-permute-start.16 = (bf16[1,1,8,128]{3,2,0,1:T(8,128)(2,1)S(1)}, bf16[1,1,8,128]{3,2,0,1:T(8,128)(2,1)S(1)}, u32[]{:S(2)}, u32[]{:S(2)}) collective-permute-start(bf16[1,1,8,128]{3,2,0,1:T(8,128)(2,1)S(1)} %get-tuple-element.16), channel_id=1, source_target_pairs={{0,32},{32,64},{64,96},{96,128},{128,160},{160,192},{192,224},{1,3... | collective-permute-start | bytes 6152 | tf_op jit(solution)/shard_map/ppermute | solution.py:17
  141.3 1.9 %collective-permute-start.17 = (bf16[1,1,8,128]{3,2,1,0:T(8,128)(2,1)S(1)}, bf16[1,1,8,128]{3,2,1,0:T(8,128)(2,1)S(1)}, u32[]{:S(2)}, u32[]{:S(2)}) collective-permute-start(bf16[1,1,8,128]{3,2,1,0:T(8,128)(2,1)S(1)} %get-tuple-element.17), channel_id=1, source_target_pairs={{32,0},{64,32},{96,64},{128,96},{160,128},{192,160},{224,192},{33,... | collective-permute-start | bytes 6152 | tf_op jit(solution)/shard_map/ppermute | solution.py:19
  143.2 5.1 %collective-permute-done.17 = bf16[1,1,8,128]{3,2,1,0:T(8,128)(2,1)S(1)} collective-permute-done((bf16[1,1,8,128]{3,2,1,0:T(8,128)(2,1)S(1)}, bf16[1,1,8,128]{3,2,1,0:T(8,128)(2,1)S(1)}, u32[]{:S(2)}, u32[]{:S(2)}) %collective-permute-start.17) | collective-permute-done | bytes 2080 | tf_op jit(solution)/shard_map/ppermute | solution.py:19
  148.3 1.9 %collective-permute-start.19 = (bf16[4,1,8,128]{3,2,0,1:T(8,128)(2,1)S(1)}, bf16[4,1,8,128]{3,2,0,1:T(8,128)(2,1)S(1)}, u32[]{:S(2)}, u32[]{:S(2)}) collective-permute-start(bf16[4,1,8,128]{3,2,0,1:T(8,128)(2,1)S(1)} %pad_maximum_fusion.4), channel_id=1, source_target_pairs={{4,0},{8,4},{12,8},{16,12},{20,16},{24,20},{28,24},{5,1},{9,5},{13... | collective-permute-start | bytes 24584 | tf_op jit(solution)/shard_map/ppermute | solution.py:19
  150.2 3.4 %collective-permute-start.18 = (bf16[4,1,8,128]{3,2,0,1:T(8,128)(2,1)S(1)}, bf16[4,1,8,128]{3,2,0,1:T(8,128)(2,1)S(1)}, u32[]{:S(2)}, u32[]{:S(2)}) collective-permute-start(bf16[4,1,8,128]{3,2,0,1:T(8,128)(2,1)S(1)} %pad_maximum_fusion.4), channel_id=1, source_target_pairs={{0,4},{4,8},{8,12},{12,16},{16,20},{20,24},{24,28},{1,5},{5,9},{9,... | collective-permute-start | bytes 24584 | tf_op jit(solution)/shard_map/ppermute | solution.py:17
  153.6 0.6 copy.50
  154.2 2.6 %collective-permute-done.18 = bf16[4,1,8,128]{3,2,0,1:T(8,128)(2,1)S(1)} collective-permute-done((bf16[4,1,8,128]{3,2,0,1:T(8,128)(2,1)S(1)}, bf16[4,1,8,128]{3,2,0,1:T(8,128)(2,1)S(1)}, u32[]{:S(2)}, u32[]{:S(2)}) %collective-permute-start.18) | collective-permute-done | bytes 8224 | tf_op jit(solution)/shard_map/ppermute | solution.py:17
  157.8 0.2 fusion.93
  158.2 0.2 fusion.97
  158.4 0.2 fusion.99
  158.6 1.0 fusion
  159.7 0.6 copy.51
  (77 shorter events, 6.9 us)
Async XLA Ops:
  0.6 38.6 %copy-start = (bf16[2,1,2,27,128,128]{5,4,3,2,1,0:T(8,128)(2,1)S(1)}, bf16[2,1,2,27,128,128]{5,4,3,2,1,0:T(8,128)(2,1)}, u32[]{:S(2)}) copy-start(bf16[2,1,2,27,128,128]{5,4,3,2,1,0:T(8,128)(2,1)} %param.5) | copy-start | bytes 10616836
  0.6 44.9 %copy-start.1 = (s32[2,1,8]{2,1,0:T(1,128)S(1)}, s32[2,1,8]{2,1,0:T(1,128)}, u32[]{:S(2)}) copy-start(s32[2,1,8]{2,1,0:T(1,128)} %param.7) | copy-start | bytes 196
  10.7 11.9 %collective-permute-start = (bf16[1,1,8,128]{3,2,0,1:T(8,128)(2,1)}, bf16[1,1,8,128]{3,2,0,1:T(8,128)(2,1)S(1)}, u32[]{:S(2)}, u32[]{:S(2)}) collective-permute-start(bf16[1,1,8,128]{3,2,0,1:T(8,128)(2,1)} %get-tuple-element.24), channel_id=1, source_target_pairs={{0,32},{32,64},{64,96},{96,128},{128,160},{160,192},{192,224},{1,3... | collective-permute-start | bytes 6152 | tf_op jit(solution)/shard_map/ppermute | solution.py:17
  18.5 7.2 %collective-permute-start.1 = (bf16[1,1,8,128]{3,2,1,0:T(8,128)(2,1)}, bf16[1,1,8,128]{3,2,1,0:T(8,128)(2,1)S(1)}, u32[]{:S(2)}, u32[]{:S(2)}) collective-permute-start(bf16[1,1,8,128]{3,2,1,0:T(8,128)(2,1)} %get-tuple-element.25), channel_id=1, source_target_pairs={{32,0},{64,32},{96,64},{128,96},{160,128},{192,160},{224,192},{33,... | collective-permute-start | bytes 6152 | tf_op jit(solution)/shard_map/ppermute | solution.py:19
  21.0 19.2 %copy-start.3 = (f32[2,1,2,128]{3,2,1,0:T(2,128)S(1)}, f32[2,1,2,128]{3,2,1,0:T(2,128)}, u32[]{:S(2)}) copy-start(f32[2,1,2,128]{3,2,1,0:T(2,128)} %param.9) | copy-start | bytes 6148
  25.7 7.1 %collective-permute-start.3 = (bf16[4,1,8,128]{3,2,0,1:T(8,128)(2,1)S(1)}, bf16[4,1,8,128]{3,2,0,1:T(8,128)(2,1)S(1)}, u32[]{:S(2)}, u32[]{:S(2)}) collective-permute-start(bf16[4,1,8,128]{3,2,0,1:T(8,128)(2,1)S(1)} %pad_maximum_fusion), channel_id=1, source_target_pairs={{4,0},{8,4},{12,8},{16,12},{20,16},{24,20},{28,24},{5,1},{9,5},{13... | collective-permute-start | bytes 24584 | tf_op jit(solution)/shard_map/ppermute | solution.py:19
  30.8 6.5 %collective-permute-start.2 = (bf16[4,1,8,128]{3,2,0,1:T(8,128)(2,1)S(1)}, bf16[4,1,8,128]{3,2,0,1:T(8,128)(2,1)S(1)}, u32[]{:S(2)}, u32[]{:S(2)}) collective-permute-start(bf16[4,1,8,128]{3,2,0,1:T(8,128)(2,1)S(1)} %pad_maximum_fusion), channel_id=1, source_target_pairs={{0,4},{4,8},{8,12},{12,16},{16,20},{20,24},{24,28},{1,5},{5,9},{9,... | collective-permute-start | bytes 24584 | tf_op jit(solution)/shard_map/ppermute | solution.py:17
  45.7 7.7 %collective-permute-start.4 = (bf16[1,1,8,128]{3,2,0,1:T(8,128)(2,1)S(1)}, bf16[1,1,8,128]{3,2,0,1:T(8,128)(2,1)S(1)}, u32[]{:S(2)}, u32[]{:S(2)}) collective-permute-start(bf16[1,1,8,128]{3,2,0,1:T(8,128)(2,1)S(1)} %get-tuple-element.22), channel_id=1, source_target_pairs={{0,32},{32,64},{64,96},{96,128},{128,160},{160,192},{192,224},{1,3... | collective-permute-start | bytes 6152 | tf_op jit(solution)/shard_map/ppermute | solution.py:17
  51.4 7.0 %collective-permute-start.5 = (bf16[1,1,8,128]{3,2,1,0:T(8,128)(2,1)S(1)}, bf16[1,1,8,128]{3,2,1,0:T(8,128)(2,1)S(1)}, u32[]{:S(2)}, u32[]{:S(2)}) collective-permute-start(bf16[1,1,8,128]{3,2,1,0:T(8,128)(2,1)S(1)} %get-tuple-element.23), channel_id=1, source_target_pairs={{32,0},{64,32},{96,64},{128,96},{160,128},{192,160},{224,192},{33,... | collective-permute-start | bytes 6152 | tf_op jit(solution)/shard_map/ppermute | solution.py:19
  58.5 5.3 %collective-permute-start.7 = (bf16[4,1,8,128]{3,2,0,1:T(8,128)(2,1)S(1)}, bf16[4,1,8,128]{3,2,0,1:T(8,128)(2,1)S(1)}, u32[]{:S(2)}, u32[]{:S(2)}) collective-permute-start(bf16[4,1,8,128]{3,2,0,1:T(8,128)(2,1)S(1)} %pad_maximum_fusion.1), channel_id=1, source_target_pairs={{4,0},{8,4},{12,8},{16,12},{20,16},{24,20},{28,24},{5,1},{9,5},{13... | collective-permute-start | bytes 24584 | tf_op jit(solution)/shard_map/ppermute | solution.py:19
  60.4 6.5 %collective-permute-start.6 = (bf16[4,1,8,128]{3,2,0,1:T(8,128)(2,1)S(1)}, bf16[4,1,8,128]{3,2,0,1:T(8,128)(2,1)S(1)}, u32[]{:S(2)}, u32[]{:S(2)}) collective-permute-start(bf16[4,1,8,128]{3,2,0,1:T(8,128)(2,1)S(1)} %pad_maximum_fusion.1), channel_id=1, source_target_pairs={{0,4},{4,8},{8,12},{12,16},{16,20},{20,24},{24,28},{1,5},{5,9},{9,... | collective-permute-start | bytes 24584 | tf_op jit(solution)/shard_map/ppermute | solution.py:17
  76.9 7.0 %collective-permute-start.8 = (bf16[1,1,8,128]{3,2,0,1:T(8,128)(2,1)S(1)}, bf16[1,1,8,128]{3,2,0,1:T(8,128)(2,1)S(1)}, u32[]{:S(2)}, u32[]{:S(2)}) collective-permute-start(bf16[1,1,8,128]{3,2,0,1:T(8,128)(2,1)S(1)} %get-tuple-element.20), channel_id=1, source_target_pairs={{0,32},{32,64},{64,96},{96,128},{128,160},{160,192},{192,224},{1,3... | collective-permute-start | bytes 6152 | tf_op jit(solution)/shard_map/ppermute | solution.py:17
  82.1 7.0 %collective-permute-start.9 = (bf16[1,1,8,128]{3,2,1,0:T(8,128)(2,1)S(1)}, bf16[1,1,8,128]{3,2,1,0:T(8,128)(2,1)S(1)}, u32[]{:S(2)}, u32[]{:S(2)}) collective-permute-start(bf16[1,1,8,128]{3,2,1,0:T(8,128)(2,1)S(1)} %get-tuple-element.21), channel_id=1, source_target_pairs={{32,0},{64,32},{96,64},{128,96},{160,128},{192,160},{224,192},{33,... | collective-permute-start | bytes 6152 | tf_op jit(solution)/shard_map/ppermute | solution.py:19
  89.1 5.3 %collective-permute-start.11 = (bf16[4,1,8,128]{3,2,0,1:T(8,128)(2,1)S(1)}, bf16[4,1,8,128]{3,2,0,1:T(8,128)(2,1)S(1)}, u32[]{:S(2)}, u32[]{:S(2)}) collective-permute-start(bf16[4,1,8,128]{3,2,0,1:T(8,128)(2,1)S(1)} %pad_maximum_fusion.2), channel_id=1, source_target_pairs={{4,0},{8,4},{12,8},{16,12},{20,16},{24,20},{28,24},{5,1},{9,5},{13... | collective-permute-start | bytes 24584 | tf_op jit(solution)/shard_map/ppermute | solution.py:19
  91.0 6.5 %collective-permute-start.10 = (bf16[4,1,8,128]{3,2,0,1:T(8,128)(2,1)S(1)}, bf16[4,1,8,128]{3,2,0,1:T(8,128)(2,1)S(1)}, u32[]{:S(2)}, u32[]{:S(2)}) collective-permute-start(bf16[4,1,8,128]{3,2,0,1:T(8,128)(2,1)S(1)} %pad_maximum_fusion.2), channel_id=1, source_target_pairs={{0,4},{4,8},{8,12},{12,16},{16,20},{20,24},{24,28},{1,5},{5,9},{9,... | collective-permute-start | bytes 24584 | tf_op jit(solution)/shard_map/ppermute | solution.py:17
  100.4 28.6 %copy-start.2 = (f32[2,1,2,128]{3,2,1,0:T(2,128)S(1)}, f32[2,1,2,128]{3,2,1,0:T(2,128)}, u32[]{:S(2)}) copy-start(f32[2,1,2,128]{3,2,1,0:T(2,128)} %param.8) | copy-start | bytes 6148
  105.8 6.8 %collective-permute-start.12 = (bf16[1,1,8,128]{3,2,0,1:T(8,128)(2,1)S(1)}, bf16[1,1,8,128]{3,2,0,1:T(8,128)(2,1)S(1)}, u32[]{:S(2)}, u32[]{:S(2)}) collective-permute-start(bf16[1,1,8,128]{3,2,0,1:T(8,128)(2,1)S(1)} %get-tuple-element.18), channel_id=1, source_target_pairs={{0,32},{32,64},{64,96},{96,128},{128,160},{160,192},{192,224},{1,3... | collective-permute-start | bytes 6152 | tf_op jit(solution)/shard_map/ppermute | solution.py:17
  110.7 7.0 %collective-permute-start.13 = (bf16[1,1,8,128]{3,2,1,0:T(8,128)(2,1)S(1)}, bf16[1,1,8,128]{3,2,1,0:T(8,128)(2,1)S(1)}, u32[]{:S(2)}, u32[]{:S(2)}) collective-permute-start(bf16[1,1,8,128]{3,2,1,0:T(8,128)(2,1)S(1)} %get-tuple-element.19), channel_id=1, source_target_pairs={{32,0},{64,32},{96,64},{128,96},{160,128},{192,160},{224,192},{33,... | collective-permute-start | bytes 6152 | tf_op jit(solution)/shard_map/ppermute | solution.py:19
  117.7 5.3 %collective-permute-start.15 = (bf16[4,1,8,128]{3,2,0,1:T(8,128)(2,1)S(1)}, bf16[4,1,8,128]{3,2,0,1:T(8,128)(2,1)S(1)}, u32[]{:S(2)}, u32[]{:S(2)}) collective-permute-start(bf16[4,1,8,128]{3,2,0,1:T(8,128)(2,1)S(1)} %pad_maximum_fusion.3), channel_id=1, source_target_pairs={{4,0},{8,4},{12,8},{16,12},{20,16},{24,20},{28,24},{5,1},{9,5},{13... | collective-permute-start | bytes 24584 | tf_op jit(solution)/shard_map/ppermute | solution.py:19
  119.6 6.5 %collective-permute-start.14 = (bf16[4,1,8,128]{3,2,0,1:T(8,128)(2,1)S(1)}, bf16[4,1,8,128]{3,2,0,1:T(8,128)(2,1)S(1)}, u32[]{:S(2)}, u32[]{:S(2)}) collective-permute-start(bf16[4,1,8,128]{3,2,0,1:T(8,128)(2,1)S(1)} %pad_maximum_fusion.3), channel_id=1, source_target_pairs={{0,4},{4,8},{8,12},{12,16},{16,20},{20,24},{24,28},{1,5},{5,9},{9,... | collective-permute-start | bytes 24584 | tf_op jit(solution)/shard_map/ppermute | solution.py:17
  136.2 7.0 %collective-permute-start.16 = (bf16[1,1,8,128]{3,2,0,1:T(8,128)(2,1)S(1)}, bf16[1,1,8,128]{3,2,0,1:T(8,128)(2,1)S(1)}, u32[]{:S(2)}, u32[]{:S(2)}) collective-permute-start(bf16[1,1,8,128]{3,2,0,1:T(8,128)(2,1)S(1)} %get-tuple-element.16), channel_id=1, source_target_pairs={{0,32},{32,64},{64,96},{96,128},{128,160},{160,192},{192,224},{1,3... | collective-permute-start | bytes 6152 | tf_op jit(solution)/shard_map/ppermute | solution.py:17
  141.3 7.0 %collective-permute-start.17 = (bf16[1,1,8,128]{3,2,1,0:T(8,128)(2,1)S(1)}, bf16[1,1,8,128]{3,2,1,0:T(8,128)(2,1)S(1)}, u32[]{:S(2)}, u32[]{:S(2)}) collective-permute-start(bf16[1,1,8,128]{3,2,1,0:T(8,128)(2,1)S(1)} %get-tuple-element.17), channel_id=1, source_target_pairs={{32,0},{64,32},{96,64},{128,96},{160,128},{192,160},{224,192},{33,... | collective-permute-start | bytes 6152 | tf_op jit(solution)/shard_map/ppermute | solution.py:19
  148.3 5.9 %collective-permute-start.19 = (bf16[4,1,8,128]{3,2,0,1:T(8,128)(2,1)S(1)}, bf16[4,1,8,128]{3,2,0,1:T(8,128)(2,1)S(1)}, u32[]{:S(2)}, u32[]{:S(2)}) collective-permute-start(bf16[4,1,8,128]{3,2,0,1:T(8,128)(2,1)S(1)} %pad_maximum_fusion.4), channel_id=1, source_target_pairs={{4,0},{8,4},{12,8},{16,12},{20,16},{24,20},{28,24},{5,1},{9,5},{13... | collective-permute-start | bytes 24584 | tf_op jit(solution)/shard_map/ppermute | solution.py:19
  150.2 6.5 %collective-permute-start.18 = (bf16[4,1,8,128]{3,2,0,1:T(8,128)(2,1)S(1)}, bf16[4,1,8,128]{3,2,0,1:T(8,128)(2,1)S(1)}, u32[]{:S(2)}, u32[]{:S(2)}) collective-permute-start(bf16[4,1,8,128]{3,2,0,1:T(8,128)(2,1)S(1)} %pad_maximum_fusion.4), channel_id=1, source_target_pairs={{0,4},{4,8},{8,12},{12,16},{16,20},{20,24},{24,28},{1,5},{5,9},{9,... | collective-permute-start | bytes 24584 | tf_op jit(solution)/shard_map/ppermute | solution.py:17
where the time goes:
time: 161 us; the launch traced here: 160 us
  starting transfers between devices  66.3 us (41%)
  waiting for transfers between devices  39.9 us (25%)
  blocking collectives  32.3 us (20%)
  matrix products  15.5 us (10%)
  local copies, waits for them, and re-layouts  3.64 us (2%)
  other arithmetic  1.62 us (1%)
    ppermute x10, starting transfers between devices, padded_2(): lax.ppermute(tail, axis, [(i, (i + 1) % count) for i in range(ends)])  44 us
    all_gather x5, blocking collectives, operator(): lax.all_gather(vector.astype(jnp.bfloat16), 'gz', axis=2, tiled=True)  32.3 us
    ppermute x10, waiting for transfers between devices, padded_2(): lax.ppermute(head, axis, [((i + 1) % count, i) for i in range(ends)])  23.5 us
    ppermute x10, starting transfers between devices, padded_2(): lax.ppermute(head, axis, [((i + 1) % count, i) for i in range(ends)])  22.3 us
    ppermute x10, waiting for transfers between devices, padded_2(): lax.ppermute(tail, axis, [(i, (i + 1) % count) for i in range(ends)])  16.4 us
    dot_general x45, matrix products, coupled_product(): jnp.einsum('xyscp,xypw->xyscw', table, column, preferred_element_type=jnp...  9.05 us
    dot_general x5, matrix products, coupled_product(): jnp.einsum('xysoj,xysoij->xysi', gathered, matrix, preferred_element_type...  5.22 us
  transfers between devices with their start and end apart: 20, of which 10 were waited for; matrix products, arithmetic and copies ran while one was open for 2% of the time, Pallas kernels for 0%

commit v1 on v0

v1 whole, which is shorter than its diff:
```python
import jax
import jax.numpy as jnp
from jax import lax
from jax.experimental import pallas as pl
from jax.experimental.pallas import tpu as pltpu
from jax.sharding import PartitionSpec as P

DEG = 4
MESH = pl.DeviceIdType.MESH

SIDES = (-1, 1, 0)
OFFSETS = [(dx, dy, dz) for dx in SIDES for dy in SIDES for dz in (1, 2, 3, 0)]
PEERS = len(OFFSETS) - 1
HALO = [(dx, dy) for dx in SIDES for dy in SIDES]


def coefficients():
    center, spread = 1.0, 0.8
    sigma = center / spread
    rho = 1.0 / sigma
    old, new = [0.0], [1.0 / center]
    for _ in range(DEG - 1):
        following = 1.0 / (2.0 * sigma - rho)
        old.append(following * rho)
        new.append(2.0 * following / spread)
        rho = following
    return old, new


def kernel(sizes, blocks_hbm, order_ref, pattern_ref, start_ref, rhs_ref, smoothed_ref, remainder_ref,
           blocks, recv, sent, tags, tag_out, select, block_sem, send_sem, recv_sem, tag_send, tag_recv):
    nx, ny, nz = sizes
    gx, gy, gz = (lax.axis_index(a) for a in ("gx", "gy", "gz"))
    wide, _, depth, width = start_ref.shape
    rows = wide * depth
    load = pltpu.make_async_copy(blocks_hbm, blocks, block_sem)
    load.start()

    def at(offset):
        dx, dy, dz = offset
        return (lax.rem(gx + (dx + nx), nx), lax.rem(gy + (dy + ny), ny), lax.rem(gz + dz, nz))

    barrier = pltpu.get_barrier_semaphore()
    for offset in OFFSETS[:PEERS]:
        pl.semaphore_signal(barrier, inc=1, device_id=at(offset), device_id_type=MESH)

    lane = lax.broadcasted_iota(jnp.int32, (8, width), 1)
    period = lane & (4 * rows - 1)
    turn = period // rows
    row = period & (rows - 1)
    below = (gz + 3 - turn) & (nz - 1)
    place = (row // depth) * 8 + below * depth + (row & (depth - 1))
    tag = jnp.zeros((8, width), jnp.float32)
    for column in range(wide):
        for slot in range(8):
            value = order_ref[column, 0, slot].astype(jnp.float32)
            tag = jnp.where(place == column * 8 + slot, value, tag)
    tag_out[...] = tag
    tags[len(HALO) - 1] = tag

    v = start_ref[...].reshape(rows, width)
    sent[0] = v.astype(jnp.bfloat16)
    pl.semaphore_wait(barrier, PEERS)

    for number, (dx, dy) in enumerate(HALO[:-1]):
        pltpu.make_async_remote_copy(
            tag_out, tags.at[number], tag_send, tag_recv, device_id=at((dx, dy, 0)), device_id_type=MESH
        ).start()

    span = 2 * width
    col = lax.broadcasted_iota(jnp.int32, (8, span), 1)
    own = lax.broadcasted_iota(jnp.int32, (8, span), 0)
    halo = col // (4 * rows)
    side_x = (halo >= 3).astype(jnp.int32) + (halo >= 6).astype(jnp.int32)
    side_y = halo - 3 * side_x
    from_x = jnp.where(side_x == 0, 1, jnp.where(side_x == 1, -1, 0))
    from_y = jnp.where(side_y == 0, 1, jnp.where(side_y == 1, -1, 0))
    inside = (
        (gx + from_x >= 0) & (gx + from_x < nx) & (gy + from_y >= 0) & (gy + from_y < ny)
        & (col < 4 * rows * len(HALO)) & (own < rows)
    )
    step_x = wide * from_x + ((col & (rows - 1)) // depth) - (own // depth)
    flat = jnp.where(inside, (step_x + 1) * 3 + from_y + 1, -1)
    flat = jnp.where((step_x < -1) | (step_x > 1), -1, flat)

    sub = lax.broadcasted_iota(jnp.int32, (8, 1), 0)
    mine = jnp.full((8, 1), -100.0, jnp.float32)
    height = lax.broadcasted_iota(jnp.int32, (8, pattern_ref.shape[-1]), 0)
    keep = jnp.zeros((8, pattern_ref.shape[-1]), jnp.int32)
    for column in range(wide):
        present = pattern_ref[column, 0]
        for slot in range(depth):
            r = column * depth + slot
            mine = jnp.where(sub == r, order_ref[column, 0, gz * depth + slot].astype(jnp.float32), mine)
            line = jnp.sum(jnp.where(height == gz * depth + slot, present, 0), axis=0, keepdims=True)
            keep = jnp.where(height == r, line, keep)

    old, new = coefficients()

    def turn_of(number, carry, first=False):
        v, smoothed, remainder = carry
        if not first:
            sent[number] = v.astype(jnp.bfloat16)
        for k, offset in enumerate(OFFSETS[:PEERS]):
            pltpu.make_async_remote_copy(
                sent.at[number], recv.at[number, pl.ds(k * rows, rows)], send_sem.at[number], recv_sem.at[number],
                device_id=at(offset), device_id_type=MESH,
            ).start()
        recv[number, pl.ds(PEERS * rows, rows)] = sent[number]
        if first:
            pltpu.make_async_copy(tags.at[pl.ds(0, len(HALO) - 1)], tags.at[pl.ds(0, len(HALO) - 1)], tag_recv).wait()
            half = lax.broadcasted_iota(jnp.int32, (8, width), 1) // (4 * rows)
            low = jnp.zeros((8, width), jnp.float32)
            for g in range(8):
                low = jnp.where(half == g, tags[g], low)
            plane = jnp.concatenate([low, tags[8]], axis=1)
            level = [plane == mine + float(c - 1) for c in range(3)]
            for o in range(27):
                chosen = (flat == o // 3) & level[o % 3]
                if o != 13:
                    chosen = chosen & (keep[:, o : o + 1] > 0)
                select[pl.ds(8 * o, 8), :] = jnp.where(chosen, 1.0, 0.0)
            load.wait()
        everything = recv.at[number, pl.ds(0, PEERS * rows)]
        pltpu.make_async_copy(everything, everything, recv_sem.at[number]).wait()
        table = select[:, 0 : 4 * rows * len(HALO)].astype(jnp.bfloat16)
        picked = jnp.dot(table, recv[number], preferred_element_type=jnp.float32).astype(jnp.bfloat16)
        pieces = []
        for r in range(rows):
            total = jnp.zeros((8, width), jnp.float32)
            for o in range(27):
                total += lax.dot_general(
                    picked[8 * o : 8 * o + 8], blocks[r * 27 + o], (((1,), (1,)), ((), ())),
                    preferred_element_type=jnp.float32,
                )
            pieces.append(total[r : r + 1])
        product = jnp.concatenate(pieces, axis=0)
        remainder = remainder - product
        smoothed = smoothed + v
        a, b = jnp.float32(old[0]), jnp.float32(new[0])
        for i in range(1, DEG):
            a = jnp.where(number == i, jnp.float32(old[i]), a)
            b = jnp.where(number == i, jnp.float32(new[i]), b)
        return (a * v + b * remainder, smoothed, remainder)

    carry = (v, jnp.zeros_like(v), rhs_ref[...].reshape(rows, width))
    carry = turn_of(0, carry, True)
    _, smoothed, remainder = lax.fori_loop(1, DEG + 1, turn_of, carry)
    smoothed_ref[...] = smoothed.reshape(smoothed_ref.shape)
    remainder_ref[...] = remainder.reshape(remainder_ref.shape)

    others = tags.at[pl.ds(0, len(HALO) - 1)]
    pltpu.make_async_copy(others, others, tag_send).wait()
    for number in range(DEG + 1):
        everything = recv.at[number, pl.ds(0, PEERS * rows)]
        pltpu.make_async_copy(everything, everything, send_sem.at[number]).wait()


def local(sizes, blocks, pattern, order, start, rhs):
    wide, _, depth, width = start.shape
    rows = wide * depth
    flat = blocks.reshape((rows * blocks.shape[3],) + blocks.shape[4:])
    vmem = pl.BlockSpec(memory_space=pltpu.VMEM)
    import functools

    return pl.pallas_call(
        functools.partial(kernel, sizes),
        out_shape=(jax.ShapeDtypeStruct(start.shape, jnp.float32),) * 2,
        in_specs=[
            pl.BlockSpec(memory_space=pl.ANY),
            pl.BlockSpec(memory_space=pltpu.SMEM),
            vmem, vmem, vmem,
        ],
        out_specs=(vmem, vmem),
        scratch_shapes=[
            pltpu.VMEM(flat.shape, jnp.bfloat16),
            pltpu.VMEM((DEG + 1, len(OFFSETS) * rows, width), jnp.bfloat16),
            pltpu.VMEM((DEG + 1, rows, width), jnp.bfloat16),
            pltpu.VMEM((len(HALO), 8, width), jnp.float32),
            pltpu.VMEM((8, width), jnp.float32),
            pltpu.VMEM((8 * 27, 2 * width), jnp.float32),
            pltpu.SemaphoreType.DMA,
            pltpu.SemaphoreType.DMA((DEG + 1,)),
            pltpu.SemaphoreType.DMA((DEG + 1,)),
            pltpu.SemaphoreType.DMA,
            pltpu.SemaphoreType.DMA,
        ],
        compiler_params=pltpu.CompilerParams(collective_id=0, has_side_effects=True),
    )(flat, order, pattern, start, rhs)


def solution(mesh):
    import functools

    in_specs = (
        P("gx", "gy", "gz", None, None, None),
        P("gx", "gy", None, None),
        P("gx", "gy", None),
        P("gx", "gy", "gz", None),
        P("gx", "gy", "gz", None),
    )
    out_specs = (P("gx", "gy", "gz", None), P("gx", "gy", "gz", None))
    sizes = tuple(mesh.shape[a] for a in ("gx", "gy", "gz"))
    return jax.shard_map(
        functools.partial(local, sizes), mesh=mesh, in_specs=in_specs, out_specs=out_specs, check_vma=False
    )
```

time: 161 us -> 54.6 us (0.34)
  the two profiles are of different devices: /device:TPU:97 before, /device:TPU:1 now
where the time goes in v1:
time: 54.6 us; the launch traced here: 54.5 us
  Pallas kernels  51.3 us (94%)
  local copies, waits for them, and re-layouts  2.48 us (5%)
  between operations  0.64 us (1%)
    pallas_call x1, Pallas kernels, local(): pl.pallas_call(functools.partial(kernel, sizes), out_shape=(jax.ShapeDtyp...  51.3 us
    unnamed x2, local copies, waits for them, and re-layouts  2.48 us

profile of v1, /device:TPU:1, one launch (start us, length us, event | category | flops | bytes accessed | tf_op | source)
XLA Modules:
  0.0 54.5 jit_solution(1192873847737190447)
XLA Ops:
  0.6 51.3 %shard_map.68 = (f32[2,1,2,128]{3,2,1,0:T(2,128)}, f32[2,1,2,128]{3,2,1,0:T(2,128)}) custom-call(bf16[108,128,128]{2,1,0:T(8,128)(2,1)} %bitcast.1, s32[2,1,8]{2,1,0:T(1,128)} %order_ref.1, s32[2,1,8,27]{3,2,1,0:T(8,128)} %pattern_ref.1, f32[2,1,2,128]{3,2,1,0:T(2,128)} %start_ref.1, f32[2,1,2,128]{3,2,1,0:T(2,128)} %rhs_ref.1), custom_call_target="tpu_custom_call" | custom-call | tf_op jit(solution)/shard_map/pallas_call | solution.py:166
  52.0 1.2 %copy.9 = f32[2,1,2,128]{3,2,1,0:T(2,128)} copy(f32[2,1,2,128]{3,2,1,0:T(2,128)} %get-tuple-element.4) | data formatting | bytes 4096
  53.2 1.2 %copy.10 = f32[2,1,2,128]{3,2,1,0:T(2,128)} copy(f32[2,1,2,128]{3,2,1,0:T(2,128)} %get-tuple-element.5) | data formatting | bytes 4096

commit v2 on v1

v2 whole, which is shorter than its diff:
```python
import functools

import jax
import jax.numpy as jnp
from jax import lax
from jax.experimental import pallas as pl
from jax.experimental.pallas import tpu as pltpu
from jax.sharding import PartitionSpec as P

DEG = 4
MESH = pl.DeviceIdType.MESH

NEAR = ((-1, 0), (1, 0), (0, -1), (0, 1), (0, 0))
FAR = ((1, 1), (-1, -1), (1, -1), (-1, 1))
TURNS = (1, 2, 3, 0)
ISSUE = (2, 1, 3, 0)
NEAR_ENTRIES = [(9 * a + 3 * b + c, 9 * d + 3 * b + c) for a, d in ((1, 1), (2, 0)) for b in range(3) for c in range(3)]
NEAR_ENTRIES += [(3 + c, 21 + c) for c in range(3)]
FAR_ENTRIES = [(3 * b + c, 18 + 3 * b + c) for b in (0, 2) for c in range(3)]


def coefficients():
    center, spread = 1.0, 0.8
    sigma = center / spread
    rho = 1.0 / sigma
    old, new = [0.0], [1.0 / center]
    for _ in range(DEG - 1):
        following = 1.0 / (2.0 * sigma - rho)
        old.append(following * rho)
        new.append(2.0 * following / spread)
        rho = following
    return old, new


def kernel(sizes, blocks_hbm, order_ref, pattern_hbm, start_hbm, rhs_hbm, out_ref,
           blocks, pattern, first, rhs, near, far, sent, tags, tag_out, near_table, far_table, masks,
           load_sem, send_sem, near_sem, far_sem, tag_send, tag_recv):
    nx, ny, nz = sizes
    gx, gy, gz = (lax.axis_index(a) for a in ("gx", "gy", "gz"))
    wide, _, depth, width = first.shape
    rows = wide * depth
    near_peers, far_peers = 4 * len(NEAR) - 1, 4 * len(FAR)

    def at(dx, dy, dz):
        return (lax.rem(gx + (dx + nx), nx), lax.rem(gy + (dy + ny), ny), lax.rem(gz + dz, nz))

    barrier = pltpu.get_barrier_semaphore()
    for dz in ISSUE:
        for dx, dy in FAR + NEAR:
            if (dx, dy, dz) != (0, 0, 0):
                pl.semaphore_signal(barrier, inc=1, device_id=at(dx, dy, dz), device_id_type=MESH)

    small = [
        pltpu.make_async_copy(a, b, load_sem.at[1 + i])
        for i, (a, b) in enumerate(((start_hbm, first), (rhs_hbm, rhs), (pattern_hbm, pattern)))
    ]
    for copy in small:
        copy.start()
    load = pltpu.make_async_copy(blocks_hbm, blocks, load_sem.at[0])
    load.start()

    lane = lax.broadcasted_iota(jnp.int32, (8, width), 1)
    own = lax.broadcasted_iota(jnp.int32, (8, width), 0)
    period = lane & (4 * rows - 1)
    row = period & (rows - 1)
    below = (gz + 3 - period // rows) & (nz - 1)
    place = (row // depth) * 8 + below * depth + (row & (depth - 1))
    tag = jnp.zeros((8, width), jnp.float32)
    for column in range(wide):
        for slot in range(8):
            value = order_ref[column, 0, slot].astype(jnp.float32)
            tag = jnp.where(place == column * 8 + slot, value, tag)
    tag_out[...] = tag

    for copy in small:
        copy.wait()
    filler = jnp.zeros((8 - rows, width), jnp.float32)
    v = jnp.concatenate([first[...].reshape(rows, width), filler], axis=0)
    remainder = jnp.concatenate([rhs[...].reshape(rows, width), filler], axis=0)
    sent[0] = v[0:rows].astype(jnp.bfloat16)

    def halo(groups):
        group = lane // (4 * rows)
        dx, dy = jnp.zeros_like(lane), jnp.zeros_like(lane)
        for g, (x, y) in enumerate(groups):
            dx = jnp.where(group == g, -x, dx)
            dy = jnp.where(group == g, -y, dy)
        inside = (gx + dx >= 0) & (gx + dx < nx) & (gy + dy >= 0) & (gy + dy < ny)
        inside = inside & (lane < 4 * rows * len(groups)) & (own < rows)
        step = wide * dx + (row // depth) - (own // depth)
        return jnp.where(inside & (step >= -1) & (step <= 1), (step + 1) * 3 + dy + 1, -1)

    mine = jnp.full((8, width), -100.0, jnp.float32)
    height = lax.broadcasted_iota(jnp.int32, (8, pattern.shape[-1]), 0)
    keep = jnp.zeros((8, pattern.shape[-1]), jnp.int32)
    for column in range(wide):
        present = pattern[column, 0]
        for slot in range(depth):
            r = column * depth + slot
            mine = jnp.where(own == r, order_ref[column, 0, gz * depth + slot].astype(jnp.float32), mine)
            line = jnp.sum(jnp.where(height == gz * depth + slot, present, 0), axis=0, keepdims=True)
            keep = jnp.where(height == r, line, keep)

    def premask(entries, groups, base):
        flat = halo(groups)
        for j, (low, high) in enumerate(entries):
            chosen = flat == jnp.where(own < depth, low // 3, high // 3)
            if low != 13:
                held = jnp.where(own[:, 0:1] < depth, keep[:, low : low + 1], keep[:, high : high + 1])
                chosen = chosen & (held > 0)
            masks[base + j] = jnp.where(chosen, 1.0, 0.0)

    premask(NEAR_ENTRIES, NEAR, 0)
    premask(FAR_ENTRIES, FAR, len(NEAR_ENTRIES))

    pl.semaphore_wait(barrier, near_peers + far_peers)

    def send(number):
        for groups, buffer, sem in ((FAR, far, far_sem), (NEAR, near, near_sem)):
            for dz in ISSUE:
                for g, (dx, dy) in enumerate(groups):
                    if (dx, dy, dz) == (0, 0, 0):
                        continue
                    slot = 4 * g + TURNS.index(dz)
                    pltpu.make_async_remote_copy(
                        sent.at[number], buffer.at[number, pl.ds(slot * rows, rows)], send_sem.at[number],
                        sem.at[number], device_id=at(dx, dy, dz), device_id_type=MESH,
                    ).start()

    everyone = FAR + NEAR
    for g, (dx, dy) in enumerate(everyone[:-1]):
        pltpu.make_async_remote_copy(
            tag_out, tags.at[g], tag_send, tag_recv, device_id=at(dx, dy, 0), device_id_type=MESH
        ).start()
    send(0)
    others = tags.at[pl.ds(0, len(everyone) - 1)]
    pltpu.make_async_copy(others, others, tag_recv).wait()
    tags[len(everyone) - 1] = tag

    def finish(entries, base, first_tag, count, table):
        plane = jnp.zeros((8, width), jnp.float32)
        for g in range(count):
            plane = jnp.where(lane // (4 * rows) == g, tags[first_tag + g], plane)
        level = [jnp.where(plane == mine + float(c - 1), 1.0, 0.0) for c in range(3)]
        parts = [masks[base + j] * level[low % 3] for j, (low, _) in enumerate(entries)]
        if len(parts) % 2:
            parts.append(jnp.zeros((8, width), jnp.float32))
        for j in range(0, len(parts), 2):
            both = jnp.concatenate(parts[j : j + 2], axis=0)
            table[pl.ds(8 * j, 16), :] = both.astype(jnp.bfloat16)

    finish(NEAR_ENTRIES, 0, len(FAR), len(NEAR), near_table)
    finish(FAR_ENTRIES, len(NEAR_ENTRIES), 0, len(FAR), far_table)
    load.wait()

    old, new = coefficients()

    def apply(table, count, buffer, entries):
        picked = jnp.dot(table[:, 0:count], buffer, preferred_element_type=jnp.float32)
        left = jnp.concatenate(
            [picked[8 * j : 8 * j + 8].astype(jnp.bfloat16) for j in range(len(entries))], axis=1
        )
        product = jnp.zeros((8, width), jnp.float32)
        for r in range(rows):
            right = jnp.concatenate([blocks[r * 27 + pair[r // depth]] for pair in entries], axis=1)
            total = lax.dot_general(left, right, (((1,), (1,)), ((), ())), preferred_element_type=jnp.float32)
            product = jnp.where(own == r, total, product)
        return product

    def turn_of(number, carry):
        v, smoothed, remainder = carry
        a, b = jnp.float32(old[0]), jnp.float32(new[0])
        for i in range(1, DEG):
            a = jnp.where(number == i, jnp.float32(old[i]), a)
            b = jnp.where(number == i, jnp.float32(new[i]), b)
        near[number, pl.ds(near_peers * rows, rows)] = sent[number]
        theirs = near.at[number, pl.ds(0, near_peers * rows)]
        pltpu.make_async_copy(theirs, theirs, near_sem.at[number]).wait()
        partial = remainder - apply(near_table, 4 * rows * len(NEAR), near[number], NEAR_ENTRIES)
        theirs = far.at[number]
        pltpu.make_async_copy(theirs, theirs, far_sem.at[number]).wait()
        remainder = partial - apply(far_table, 4 * rows * len(FAR), far[number], FAR_ENTRIES)
        following = a * v + b * remainder

        @pl.when(number < DEG)
        def _():
            sent[number + 1] = following[0:rows].astype(jnp.bfloat16)
            send(number + 1)

        return following, smoothed + v, remainder

    _, smoothed, remainder = lax.fori_loop(0, DEG + 1, turn_of, (v, jnp.zeros_like(v), remainder))
    out_ref[0] = smoothed[0:rows].reshape(first.shape)
    out_ref[1] = remainder[0:rows].reshape(first.shape)

    pltpu.make_async_copy(others, others, tag_send).wait()

    def drain(number, carry):
        theirs = near.at[number, pl.ds(0, near_peers * rows)]
        pltpu.make_async_copy(theirs, theirs, send_sem.at[number]).wait()
        theirs = far.at[number]
        pltpu.make_async_copy(theirs, theirs, send_sem.at[number]).wait()
        return carry

    lax.fori_loop(0, DEG + 1, drain, 0)


def split(both_ref, smoothed_ref, remainder_ref):
    smoothed_ref[...] = both_ref[0]
    remainder_ref[...] = both_ref[1]


def local(sizes, blocks, pattern, order, start, rhs):
    wide, _, depth, width = start.shape
    rows = wide * depth
    flat = blocks.reshape((rows * blocks.shape[3],) + blocks.shape[4:])
    vmem = pl.BlockSpec(memory_space=pltpu.VMEM)
    anywhere = pl.BlockSpec(memory_space=pl.ANY)
    near_blocks, far_blocks = (len(NEAR_ENTRIES) + 1) // 2, (len(FAR_ENTRIES) + 1) // 2
    both = pl.pallas_call(
        functools.partial(kernel, sizes),
        out_shape=jax.ShapeDtypeStruct((2,) + start.shape, jnp.float32),
        in_specs=[anywhere, pl.BlockSpec(memory_space=pltpu.SMEM), anywhere, anywhere, anywhere],
        out_specs=vmem,
        scratch_shapes=[
            pltpu.VMEM(flat.shape, jnp.bfloat16),
            pltpu.VMEM(pattern.shape, jnp.int32),
            pltpu.VMEM(start.shape, jnp.float32),
            pltpu.VMEM(start.shape, jnp.float32),
            pltpu.VMEM((DEG + 1, 4 * rows * len(NEAR), width), jnp.bfloat16),
            pltpu.VMEM((DEG + 1, 4 * rows * len(FAR), width), jnp.bfloat16),
            pltpu.VMEM((DEG + 1, rows, width), jnp.bfloat16),
            pltpu.VMEM((len(NEAR) + len(FAR), 8, width), jnp.float32),
            pltpu.VMEM((8, width), jnp.float32),
            pltpu.VMEM((16 * near_blocks, width), jnp.bfloat16),
            pltpu.VMEM((16 * far_blocks, width), jnp.bfloat16),
            pltpu.VMEM((len(NEAR_ENTRIES) + len(FAR_ENTRIES), 8, width), jnp.float32),
            pltpu.SemaphoreType.DMA((4,)),
            pltpu.SemaphoreType.DMA((DEG + 1,)),
            pltpu.SemaphoreType.DMA((DEG + 1,)),
            pltpu.SemaphoreType.DMA((DEG + 1,)),
            pltpu.SemaphoreType.DMA,
            pltpu.SemaphoreType.DMA,
        ],
        compiler_params=pltpu.CompilerParams(collective_id=0, has_side_effects=True),
    )(flat, order, pattern, start, rhs)
    piece = jax.ShapeDtypeStruct(start.shape, jnp.float32)
    return pl.pallas_call(split, out_shape=(piece, piece), in_specs=[vmem], out_specs=(vmem, vmem))(both)


def solution(mesh):
    in_specs = (
        P("gx", "gy", "gz", None, None, None),
        P("gx", "gy", None, None),
        P("gx", "gy", None),
        P("gx", "gy", "gz", None),
        P("gx", "gy", "gz", None),
    )
    out_specs = (P("gx", "gy", "gz", None), P("gx", "gy", "gz", None))
    sizes = tuple(mesh.shape[a] for a in ("gx", "gy", "gz"))
    return jax.shard_map(
        functools.partial(local, sizes), mesh=mesh, in_specs=in_specs, out_specs=out_specs, check_vma=False
    )
```

time: 54.6 us -> 45.7 us (0.84)
  Pallas kernels: 51.3 us -> 44.9 us
  local copies, waits for them, and re-layouts: 2.48 us -> 0 us
    pallas_call x1 -> x2, Pallas kernels: 51.3 us -> 44.9 us  [the longest x1 43.6 us: local(): pl.pallas_call(functools.partial(kernel, sizes), out_shape=jax.ShapeDtype...]
    unnamed x2 -> x0, local copies, waits for them, and re-layouts: 2.48 us -> none
where the time goes in v2:
time: 45.7 us; the launch traced here: 45.5 us
  Pallas kernels  44.9 us (98%)
  between operations  0.64 us (1%)
    pallas_call x1, Pallas kernels, local(): pl.pallas_call(functools.partial(kernel, sizes), out_shape=jax.ShapeDtype...  43.6 us
    pallas_call x1, Pallas kernels, local(): pl.pallas_call(split, out_shape=(piece, piece), in_specs=[vmem], out_spec...  1.27 us

profile of v2, /device:TPU:1, one launch (start us, length us, event | category | flops | bytes accessed | tf_op | source)
XLA Modules:
  0.0 45.5 jit_solution(7090715709458598304)
XLA Ops:
  0.6 43.6 %shard_map.68.both_ref = f32[2,2,1,2,128]{4,3,2,1,0:T(2,128)} custom-call(bf16[108,128,128]{2,1,0:T(8,128)(2,1)} %bitcast.1, s32[2,1,8]{2,1,0:T(1,128)} %order_ref.1, s32[2,1,8,27]{3,2,1,0:T(8,128)} %pattern_hbm.1, f32[2,1,2,128]{3,2,1,0:T(2,128)} %start_hbm.1, f32[2,1,2,128]{3,2,1,0:T(2,128)} %rhs_hbm.1), custom_call_target="tpu_custom_call" | custom-call | tf_op jit(solution)/shard_map/pallas_call | solution.py:220
  44.3 1.3 %shard_map.69 = (f32[2,1,2,128]{3,2,1,0:T(2,128)}, f32[2,1,2,128]{3,2,1,0:T(2,128)}) custom-call(f32[2,2,1,2,128]{4,3,2,1,0:T(2,128)} %shard_map.68.both_ref), custom_call_target="tpu_custom_call" | custom-call | tf_op jit(solution)/shard_map/pallas_call | solution.py:248

commit v3 on v2

--- a/solution.py
+++ b/solution.py
@@ -32,8 +32,8 @@
     return old, new
 
 
-def kernel(sizes, blocks_hbm, order_ref, pattern_hbm, start_hbm, rhs_hbm, out_ref,
-           blocks, pattern, first, rhs, near, far, sent, tags, tag_out, near_table, far_table, masks,
+def kernel(sizes, blocks_hbm, order_hbm, pattern_hbm, start_hbm, rhs_hbm, out_ref,
+           blocks, order_ref, pattern, first, rhs, near, far, sent, tags, tag_out, near_table, far_table, masks,
            load_sem, send_sem, near_sem, far_sem, tag_send, tag_recv):
     nx, ny, nz = sizes
     gx, gy, gz = (lax.axis_index(a) for a in ("gx", "gy", "gz"))
@@ -52,13 +52,14 @@
 
     small = [
         pltpu.make_async_copy(a, b, load_sem.at[1 + i])
-        for i, (a, b) in enumerate(((start_hbm, first), (rhs_hbm, rhs), (pattern_hbm, pattern)))
+        for i, (a, b) in enumerate(((order_hbm, order_ref), (start_hbm, first), (rhs_hbm, rhs), (pattern_hbm, pattern)))
     ]
     for copy in small:
         copy.start()
     load = pltpu.make_async_copy(blocks_hbm, blocks, load_sem.at[0])
     load.start()
 
+    small[0].wait()
     lane = lax.broadcasted_iota(jnp.int32, (8, width), 1)
     own = lax.broadcasted_iota(jnp.int32, (8, width), 0)
     period = lane & (4 * rows - 1)
@@ -72,7 +73,7 @@
             tag = jnp.where(place == column * 8 + slot, value, tag)
     tag_out[...] = tag
 
-    for copy in small:
+    for copy in small[1:]:
         copy.wait()
     filler = jnp.zeros((8 - rows, width), jnp.float32)
     v = jnp.concatenate([first[...].reshape(rows, width), filler], axis=0)
@@ -219,11 +220,12 @@
     near_blocks, far_blocks = (len(NEAR_ENTRIES) + 1) // 2, (len(FAR_ENTRIES) + 1) // 2
     both = pl.pallas_call(
         functools.partial(kernel, sizes),
-        out_shape=jax.ShapeDtypeStruct((2,) + start.shape, jnp.float32),
-        in_specs=[anywhere, pl.BlockSpec(memory_space=pltpu.SMEM), anywhere, anywhere, anywhere],
+        out_shape=pltpu.VMEM((2,) + start.shape, jnp.float32),
+        in_specs=[anywhere, anywhere, anywhere, anywhere, anywhere],
         out_specs=vmem,
         scratch_shapes=[
             pltpu.VMEM(flat.shape, jnp.bfloat16),
+            pltpu.SMEM(order.shape, jnp.int32),
             pltpu.VMEM(pattern.shape, jnp.int32),
             pltpu.VMEM(start.shape, jnp.float32),
             pltpu.VMEM(start.shape, jnp.float32),
@@ -235,7 +237,7 @@
             pltpu.VMEM((16 * near_blocks, width), jnp.bfloat16),
             pltpu.VMEM((16 * far_blocks, width), jnp.bfloat16),
             pltpu.VMEM((len(NEAR_ENTRIES) + len(FAR_ENTRIES), 8, width), jnp.float32),
-            pltpu.SemaphoreType.DMA((4,)),
+            pltpu.SemaphoreType.DMA((5,)),
             pltpu.SemaphoreType.DMA((DEG + 1,)),
             pltpu.SemaphoreType.DMA((DEG + 1,)),
             pltpu.SemaphoreType.DMA((DEG + 1,)),
@@ -244,6 +246,7 @@
         ],
         compiler_params=pltpu.CompilerParams(collective_id=0, has_side_effects=True),
     )(flat, order, pattern, start, rhs)
+    both = pltpu.with_memory_space_constraint(both, pltpu.VMEM)
     piece = jax.ShapeDtypeStruct(start.shape, jnp.float32)
     return pl.pallas_call(split, out_shape=(piece, piece), in_specs=[vmem], out_specs=(vmem, vmem))(both)
 

time: 45.7 us -> 43.6 us (0.954)
  Pallas kernels: 44.9 us -> 42.9 us
    pallas_call x1, Pallas kernels: 43.6 us -> 42.3 us  [local(): pl.pallas_call(functools.partial(kernel, sizes), out_shape=pltpu.VMEM((2,...]
    pallas_call x1, Pallas kernels: 1.27 us -> 0.59 us  [local(): pl.pallas_call(split, out_shape=(piece, piece), in_specs=[vmem], out_spec...]
where the time goes in v3:
time: 43.6 us
  Pallas kernels  42.9 us (98%)
  between operations  0.64 us (1%)
    pallas_call x1, Pallas kernels, local(): pl.pallas_call(functools.partial(kernel, sizes), out_shape=pltpu.VMEM((2,...  42.3 us

profile of v3, /device:TPU:1, one launch (start us, length us, event | category | flops | bytes accessed | tf_op | source)
XLA Modules:
  0.0 43.6 jit_solution(17862990278152737769)
XLA Ops:
  0.6 42.3 %shard_map.68.both_ref = f32[2,2,1,2,128]{4,3,2,1,0:T(2,128)S(1)} custom-call(bf16[108,128,128]{2,1,0:T(8,128)(2,1)} %bitcast.1, s32[2,1,8]{2,1,0:T(1,128)} %order_hbm.1, s32[2,1,8,27]{3,2,1,0:T(8,128)} %pattern_hbm.1, f32[2,1,2,128]{3,2,1,0:T(2,128)} %start_hbm.1, f32[2,1,2,128]{3,2,1,0:T(2,128)} %rhs_hbm.1), custom_call_target="tpu_custom_call" | custom-call | tf_op jit(solution)/shard_map/pallas_call | solution.py:221
  43.0 0.6 %shard_map.69 = (f32[2,1,2,128]{3,2,1,0:T(2,128)}, f32[2,1,2,128]{3,2,1,0:T(2,128)}) custom-call(f32[2,2,1,2,128]{4,3,2,1,0:T(2,128)S(1)} %shard_map.68.both_ref), custom_call_target="tpu_custom_call" | custom-call | tf_op jit(solution)/shard_map/pallas_call | solution.py:251

commit v4 on v3

--- a/solution.py
+++ b/solution.py
@@ -33,7 +33,7 @@
 
 
 def kernel(sizes, blocks_hbm, order_hbm, pattern_hbm, start_hbm, rhs_hbm, out_ref,
-           blocks, order_ref, pattern, first, rhs, near, far, sent, tags, tag_out, near_table, far_table, masks,
+           blocks, turned, order_ref, pattern, first, rhs, near, far, sent, tags, tag_out, near_table, far_table, masks,
            load_sem, send_sem, near_sem, far_sem, tag_send, tag_recv):
     nx, ny, nz = sizes
     gx, gy, gz = (lax.axis_index(a) for a in ("gx", "gy", "gz"))
@@ -134,6 +134,19 @@
             tag_out, tags.at[g], tag_send, tag_recv, device_id=at(dx, dy, 0), device_id_type=MESH
         ).start()
     send(0)
+
+    load.wait()
+    unit = lax.broadcasted_iota(jnp.int32, (width, width), 0) == lax.broadcasted_iota(jnp.int32, (width, width), 1)
+    unit = jnp.where(unit, 1.0, 0.0).astype(jnp.bfloat16)
+
+    def turn_block(step, carry):
+        for k in range(6):
+            block = blocks[6 * step + k]
+            flipped = block.T
+            turned[6 * step + k] = flipped.astype(jnp.bfloat16)
+        return carry
+
+    lax.fori_loop(0, rows * 27 // 6, turn_block, 0)
     others = tags.at[pl.ds(0, len(everyone) - 1)]
     pltpu.make_async_copy(others, others, tag_recv).wait()
     tags[len(everyone) - 1] = tag
@@ -152,7 +165,6 @@
 
     finish(NEAR_ENTRIES, 0, len(FAR), len(NEAR), near_table)
     finish(FAR_ENTRIES, len(NEAR_ENTRIES), 0, len(FAR), far_table)
-    load.wait()
 
     old, new = coefficients()
 
@@ -162,10 +174,17 @@
             [picked[8 * j : 8 * j + 8].astype(jnp.bfloat16) for j in range(len(entries))], axis=1
         )
         product = jnp.zeros((8, width), jnp.float32)
-        for r in range(rows):
-            right = jnp.concatenate([blocks[r * 27 + pair[r // depth]] for pair in entries], axis=1)
-            total = lax.dot_general(left, right, (((1,), (1,)), ((), ())), preferred_element_type=jnp.float32)
-            product = jnp.where(own == r, total, product)
+        for r in range(0, rows, depth):
+            right = jnp.concatenate(
+                [
+                    jnp.concatenate([turned[(r + s) * 27 + pair[r // depth]] for s in range(depth)], axis=1)
+                    for pair in entries
+                ],
+                axis=0,
+            )
+            total = jnp.dot(left, right, preferred_element_type=jnp.float32)
+            for s in range(depth):
+                product = jnp.where(own == r + s, total[:, s * width : (s + 1) * width], product)
         return product
 
     def turn_of(number, carry):
@@ -224,6 +243,7 @@
         in_specs=[anywhere, anywhere, anywhere, anywhere, anywhere],
         out_specs=vmem,
         scratch_shapes=[
+            pltpu.VMEM(flat.shape, jnp.bfloat16),
             pltpu.VMEM(flat.shape, jnp.bfloat16),
             pltpu.SMEM(order.shape, jnp.int32),
             pltpu.VMEM(pattern.shape, jnp.int32),

time: 43.6 us -> 42.4 us (0.972)
  Pallas kernels: 42.9 us -> 41.7 us
    pallas_call x1, Pallas kernels: 42.3 us -> 41.1 us  [local(): pl.pallas_call(functools.partial(kernel, sizes), out_shape=pltpu.VMEM((2,...]
where the time goes in v4:
time: 42.4 us; the launch traced here: 42.3 us
  Pallas kernels  41.7 us (98%)
  between operations  0.64 us (2%)
    pallas_call x1, Pallas kernels, local(): pl.pallas_call(functools.partial(kernel, sizes), out_shape=pltpu.VMEM((2,...  41.1 us

profile of v4, /device:TPU:1, one launch (start us, length us, event | category | flops | bytes accessed | tf_op | source)
XLA Modules:
  0.0 42.3 jit_solution(12891609400945030450)
XLA Ops:
  0.6 41.1 %shard_map.68.both_ref = f32[2,2,1,2,128]{4,3,2,1,0:T(2,128)S(1)} custom-call(bf16[108,128,128]{2,1,0:T(8,128)(2,1)} %bitcast.1, s32[2,1,8]{2,1,0:T(1,128)} %order_hbm.1, s32[2,1,8,27]{3,2,1,0:T(8,128)} %pattern_hbm.1, f32[2,1,2,128]{3,2,1,0:T(2,128)} %start_hbm.1, f32[2,1,2,128]{3,2,1,0:T(2,128)} %rhs_hbm.1), custom_call_target="tpu_custom_call" | custom-call | tf_op jit(solution)/shard_map/pallas_call | solution.py:240
  41.8 0.6 %shard_map.69 = (f32[2,1,2,128]{3,2,1,0:T(2,128)}, f32[2,1,2,128]{3,2,1,0:T(2,128)}) custom-call(f32[2,2,1,2,128]{4,3,2,1,0:T(2,128)S(1)} %shard_map.68.both_ref), custom_call_target="tpu_custom_call" | custom-call | tf_op jit(solution)/shard_map/pallas_call | solution.py:271

commit v5 on v4

--- a/solution.py
+++ b/solution.py
@@ -33,7 +33,7 @@
 
 
 def kernel(sizes, blocks_hbm, order_hbm, pattern_hbm, start_hbm, rhs_hbm, out_ref,
-           blocks, turned, order_ref, pattern, first, rhs, near, far, sent, tags, tag_out, near_table, far_table, masks,
+           blocks, turned, order_ref, pattern, first, rhs, near, far, sent, tags, tag_out, near_table, masks, far_rows, spots, spot_of,
            load_sem, send_sem, near_sem, far_sem, tag_send, tag_recv):
     nx, ny, nz = sizes
     gx, gy, gz = (lax.axis_index(a) for a in ("gx", "gy", "gz"))
@@ -164,17 +164,44 @@
             table[pl.ds(8 * j, 16), :] = both.astype(jnp.bfloat16)
 
     finish(NEAR_ENTRIES, 0, len(FAR), len(NEAR), near_table)
-    finish(FAR_ENTRIES, len(NEAR_ENTRIES), 0, len(FAR), far_table)
+    plane = jnp.zeros((8, width), jnp.float32)
+    for g in range(len(FAR)):
+        plane = jnp.where(lane // (4 * rows) == g, tags[g], plane)
+    place = jnp.zeros((8, width), jnp.int32)
+    for j, (low, _) in enumerate(FAR_ENTRIES):
+        chosen = (masks[len(NEAR_ENTRIES) + j] > 0) & (plane == mine + float(low % 3 - 1))
+        spot = jnp.max(jnp.where(chosen, (lane + 8).astype(jnp.float32), 0.0), axis=1, keepdims=True)
+        place = jnp.where(lane == j, spot.astype(jnp.int32), place)
+    spots[...] = place
+    far_rows[pl.ds(0, 8), :] = jnp.zeros((8, width), jnp.float32)
+    to_scalars = pltpu.make_async_copy(spots, spot_of, load_sem.at[1])
+    to_scalars.start()
 
     old, new = coefficients()
 
-    def apply(table, count, buffer, entries):
-        picked = jnp.dot(table[:, 0:count], buffer, preferred_element_type=jnp.float32)
-        left = jnp.concatenate(
-            [picked[8 * j : 8 * j + 8].astype(jnp.bfloat16) for j in range(len(entries))], axis=1
-        )
+    def near_rows(number):
+        picked = jnp.dot(near_table[:, 0 : 4 * rows * len(NEAR)], near[number], preferred_element_type=jnp.float32)
+        parts = [picked[8 * j : 8 * j + 8].astype(jnp.bfloat16) for j in range(len(NEAR_ENTRIES))]
+        return [jnp.concatenate(parts, axis=1)] * (rows // depth)
+
+    def diagonal_rows(number):
+        far_rows[pl.ds(8, 4 * rows * len(FAR)), :] = far[number].astype(jnp.float32)
+        lefts = []
+        last = far_rows.shape[0] - 1
+        for r in range(0, rows, depth):
+            parts = []
+            for j in range(len(FAR_ENTRIES)):
+                part = jnp.broadcast_to(far_rows[pl.ds(jnp.clip(spot_of[r, j], 0, last), 1), :], (8, width))
+                for s in range(1, depth):
+                    line = jnp.broadcast_to(far_rows[pl.ds(jnp.clip(spot_of[r + s, j], 0, last), 1), :], (8, width))
+                    part = jnp.where(own == r + s, line, part)
+                parts.append(part.astype(jnp.bfloat16))
+            lefts.append(jnp.concatenate(parts, axis=1))
+        return lefts
+
+    def apply(lefts, entries):
         product = jnp.zeros((8, width), jnp.float32)
-        for r in range(0, rows, depth):
+        for left, r in zip(lefts, range(0, rows, depth)):
             right = jnp.concatenate(
                 [
                     jnp.concatenate([turned[(r + s) * 27 + pair[r // depth]] for s in range(depth)], axis=1)
@@ -196,10 +223,10 @@
         near[number, pl.ds(near_peers * rows, rows)] = sent[number]
         theirs = near.at[number, pl.ds(0, near_peers * rows)]
         pltpu.make_async_copy(theirs, theirs, near_sem.at[number]).wait()
-        partial = remainder - apply(near_table, 4 * rows * len(NEAR), near[number], NEAR_ENTRIES)
+        partial = remainder - apply(near_rows(number), NEAR_ENTRIES)
         theirs = far.at[number]
         pltpu.make_async_copy(theirs, theirs, far_sem.at[number]).wait()
-        remainder = partial - apply(far_table, 4 * rows * len(FAR), far[number], FAR_ENTRIES)
+        remainder = partial - apply(diagonal_rows(number), FAR_ENTRIES)
         following = a * v + b * remainder
 
         @pl.when(number < DEG)
@@ -209,6 +236,7 @@
 
         return following, smoothed + v, remainder
 
+    to_scalars.wait()
     _, smoothed, remainder = lax.fori_loop(0, DEG + 1, turn_of, (v, jnp.zeros_like(v), remainder))
     out_ref[0] = smoothed[0:rows].reshape(first.shape)
     out_ref[1] = remainder[0:rows].reshape(first.shape)
@@ -225,9 +253,14 @@
     lax.fori_loop(0, DEG + 1, drain, 0)
 
 
-def split(both_ref, smoothed_ref, remainder_ref):
-    smoothed_ref[...] = both_ref[0]
-    remainder_ref[...] = both_ref[1]
+def split(both_ref, smoothed_hbm, remainder_hbm, sem):
+    copies = [
+        pltpu.make_async_copy(both_ref.at[i], out, sem.at[i]) for i, out in enumerate((smoothed_hbm, remainder_hbm))
+    ]
+    for copy in copies:
+        copy.start()
+    for copy in copies:
+        copy.wait()
 
 
 def local(sizes, blocks, pattern, order, start, rhs):
@@ -236,7 +269,7 @@
     flat = blocks.reshape((rows * blocks.shape[3],) + blocks.shape[4:])
     vmem = pl.BlockSpec(memory_space=pltpu.VMEM)
     anywhere = pl.BlockSpec(memory_space=pl.ANY)
-    near_blocks, far_blocks = (len(NEAR_ENTRIES) + 1) // 2, (len(FAR_ENTRIES) + 1) // 2
+    near_blocks = (len(NEAR_ENTRIES) + 1) // 2
     both = pl.pallas_call(
         functools.partial(kernel, sizes),
         out_shape=pltpu.VMEM((2,) + start.shape, jnp.float32),
@@ -255,8 +288,10 @@
             pltpu.VMEM((len(NEAR) + len(FAR), 8, width), jnp.float32),
             pltpu.VMEM((8, width), jnp.float32),
             pltpu.VMEM((16 * near_blocks, width), jnp.bfloat16),
-            pltpu.VMEM((16 * far_blocks, width), jnp.bfloat16),
             pltpu.VMEM((len(NEAR_ENTRIES) + len(FAR_ENTRIES), 8, width), jnp.float32),
+            pltpu.VMEM((8 + 4 * rows * len(FAR), width), jnp.float32),
+            pltpu.VMEM((8, width), jnp.int32),
+            pltpu.SMEM((8, width), jnp.int32),
             pltpu.SemaphoreType.DMA((5,)),
             pltpu.SemaphoreType.DMA((DEG + 1,)),
             pltpu.SemaphoreType.DMA((DEG + 1,)),
@@ -268,7 +303,13 @@
     )(flat, order, pattern, start, rhs)
     both = pltpu.with_memory_space_constraint(both, pltpu.VMEM)
     piece = jax.ShapeDtypeStruct(start.shape, jnp.float32)
-    return pl.pallas_call(split, out_shape=(piece, piece), in_specs=[vmem], out_specs=(vmem, vmem))(both)
+    return pl.pallas_call(
+        split,
+        out_shape=(piece, piece),
+        in_specs=[vmem],
+        out_specs=(anywhere, anywhere),
+        scratch_shapes=[pltpu.SemaphoreType.DMA((2,))],
+    )(both)
 
 
 def solution(mesh):

time: 42.4 us -> 42.3 us (level)
  no operation moved by 1% of the time
where the time goes in v5:
time: 42.3 us
  Pallas kernels  41.6 us (98%)
  between operations  0.64 us (2%)
    pallas_call x1, Pallas kernels, local(): pl.pallas_call(functools.partial(kernel, sizes), out_shape=pltpu.VMEM((2,...  41 us

profile of v5, /device:TPU:1, one launch (start us, length us, event | category | flops | bytes accessed | tf_op | source)
XLA Modules:
  0.0 42.3 jit_solution(11102612510128568669)
XLA Ops:
  0.6 41.0 %shard_map.68.both_ref = f32[2,2,1,2,128]{4,3,2,1,0:T(2,128)S(1)} custom-call(bf16[108,128,128]{2,1,0:T(8,128)(2,1)} %bitcast.1, s32[2,1,8]{2,1,0:T(1,128)} %order_hbm.1, s32[2,1,8,27]{3,2,1,0:T(8,128)} %pattern_hbm.1, f32[2,1,2,128]{3,2,1,0:T(2,128)} %start_hbm.1, f32[2,1,2,128]{3,2,1,0:T(2,128)} %rhs_hbm.1), custom_call_target="tpu_custom_call" | custom-call | tf_op jit(solution)/shard_map/pallas_call | solution.py:273
  41.7 0.6 %shard_map.69 = (f32[2,1,2,128]{3,2,1,0:T(2,128)}, f32[2,1,2,128]{3,2,1,0:T(2,128)}) custom-call(f32[2,2,1,2,128]{4,3,2,1,0:T(2,128)S(1)} %shard_map.68.both_ref), custom_call_target="tpu_custom_call" | custom-call | tf_op jit(solution)/shard_map/pallas_call | solution.py:306

commit v6 on v5

--- a/solution.py
+++ b/solution.py
@@ -179,40 +179,69 @@
 
     old, new = coefficients()
 
-    def near_rows(number):
-        picked = jnp.dot(near_table[:, 0 : 4 * rows * len(NEAR)], near[number], preferred_element_type=jnp.float32)
-        parts = [picked[8 * j : 8 * j + 8].astype(jnp.bfloat16) for j in range(len(NEAR_ENTRIES))]
-        return [jnp.concatenate(parts, axis=1)] * (rows // depth)
-
-    def diagonal_rows(number):
-        far_rows[pl.ds(8, 4 * rows * len(FAR)), :] = far[number].astype(jnp.float32)
-        lefts = []
-        last = far_rows.shape[0] - 1
-        for r in range(0, rows, depth):
-            parts = []
-            for j in range(len(FAR_ENTRIES)):
-                part = jnp.broadcast_to(far_rows[pl.ds(jnp.clip(spot_of[r, j], 0, last), 1), :], (8, width))
-                for s in range(1, depth):
-                    line = jnp.broadcast_to(far_rows[pl.ds(jnp.clip(spot_of[r + s, j], 0, last), 1), :], (8, width))
-                    part = jnp.where(own == r + s, line, part)
-                parts.append(part.astype(jnp.bfloat16))
-            lefts.append(jnp.concatenate(parts, axis=1))
-        return lefts
-
-    def apply(lefts, entries):
+    def weights(entries, r, first):
+        pairs = entries[first : first + 2]
+        blocks_of = [
+            jnp.concatenate([turned[(r + s) * 27 + pair[r // depth]] for s in range(depth)], axis=1) for pair in pairs
+        ]
+        if len(pairs) == 1:
+            blocks_of.append(jnp.zeros((width, 2 * width), jnp.bfloat16))
+        return jnp.concatenate(blocks_of, axis=0)
+
+    def own_rows(totals):
         product = jnp.zeros((8, width), jnp.float32)
-        for left, r in zip(lefts, range(0, rows, depth)):
-            right = jnp.concatenate(
-                [
-                    jnp.concatenate([turned[(r + s) * 27 + pair[r // depth]] for s in range(depth)], axis=1)
-                    for pair in entries
-                ],
-                axis=0,
-            )
-            total = jnp.dot(left, right, preferred_element_type=jnp.float32)
+        for total, r in zip(totals, range(0, rows, depth)):
             for s in range(depth):
                 product = jnp.where(own == r + s, total[:, s * width : (s + 1) * width], product)
         return product
+
+    def nearby(number, picked_0, unit_0, unit_1):
+        seen = near[number]
+        seen = jnp.concatenate([seen, jnp.zeros((2 * width - seen.shape[0], width), jnp.bfloat16)], axis=0)
+        pltpu.matmul_push_rhs(jnp.concatenate([seen, jnp.zeros_like(seen)], axis=1), 0, 0)
+        units = list(zip((unit_0, unit_1), range(0, rows, depth)))
+        pltpu.matmul_push_rhs(weights(NEAR_ENTRIES, units[1][1], 0), 0, 1)
+        table = near_table[...]
+        pltpu.matmul_acc_lhs(picked_0, jnp.concatenate([table, jnp.zeros_like(table)], axis=1), 0)
+        pltpu.matmul_push_rhs(weights(NEAR_ENTRIES, units[0][1], 0), 0, 0)
+        picked = pltpu.matmul_pop(picked_0)[:, 0:width]
+        chunks = range(0, len(NEAR_ENTRIES), 2)
+        for n, first in enumerate(chunks):
+            left = jnp.concatenate([picked[8 * first : 8 * first + 8], picked[8 * first + 8 : 8 * first + 16]], axis=1)
+            left = jnp.concatenate([left, jnp.zeros_like(left)], axis=0).astype(jnp.bfloat16)
+            for i, (acc, r) in enumerate(units):
+                if n + 1 < len(chunks):
+                    pltpu.matmul_push_rhs(weights(NEAR_ENTRIES, r, first + 2), (n + 1) % 2, i)
+                pltpu.matmul_acc_lhs(acc, left, n % 2)
+        return own_rows([pltpu.matmul_pop(acc)[0:8] for acc, _ in units])
+
+    def diagonal_row(r, j):
+        last = far_rows.shape[0] - 1
+        part = jnp.broadcast_to(far_rows[pl.ds(jnp.clip(spot_of[r, j], 0, last), 1), :], (8, width))
+        for s in range(1, depth):
+            line = jnp.broadcast_to(far_rows[pl.ds(jnp.clip(spot_of[r + s, j], 0, last), 1), :], (8, width))
+            part = jnp.where(own == r + s, line, part)
+        return part
+
+    def diagonal_left(r, first):
+        left = jnp.concatenate([diagonal_row(r, first), diagonal_row(r, first + 1)], axis=1)
+        return jnp.concatenate([left, jnp.zeros_like(left)], axis=0).astype(jnp.bfloat16)
+
+    def diagonal(number, unit_0, unit_1):
+        units = list(zip((unit_0, unit_1), range(0, rows, depth)))
+        for i, (_, r) in enumerate(units):
+            pltpu.matmul_push_rhs(weights(FAR_ENTRIES, r, 0), 0, i)
+            pltpu.matmul_push_rhs(weights(FAR_ENTRIES, r, 2), 1, i)
+        theirs = far.at[number]
+        pltpu.make_async_copy(theirs, theirs, far_sem.at[number]).wait()
+        far_rows[pl.ds(8, 4 * rows * len(FAR)), :] = far[number].astype(jnp.float32)
+        for i, (acc, r) in enumerate(units):
+            pltpu.matmul_acc_lhs(acc, diagonal_left(r, 0), 0)
+            pltpu.matmul_push_rhs(weights(FAR_ENTRIES, r, 4), 0, i)
+        for i, (acc, r) in enumerate(units):
+            pltpu.matmul_acc_lhs(acc, diagonal_left(r, 2), 1)
+            pltpu.matmul_acc_lhs(acc, diagonal_left(r, 4), 0)
+        return own_rows([pltpu.matmul_pop(acc)[0:8] for acc, _ in units])
 
     def turn_of(number, carry):
         v, smoothed, remainder = carry
@@ -223,10 +252,17 @@
         near[number, pl.ds(near_peers * rows, rows)] = sent[number]
         theirs = near.at[number, pl.ds(0, near_peers * rows)]
         pltpu.make_async_copy(theirs, theirs, near_sem.at[number]).wait()
-        partial = remainder - apply(near_rows(number), NEAR_ENTRIES)
-        theirs = far.at[number]
-        pltpu.make_async_copy(theirs, theirs, far_sem.at[number]).wait()
-        remainder = partial - apply(diagonal_rows(number), FAR_ENTRIES)
+        partial = remainder - pl.run_scoped(
+            functools.partial(nearby, number),
+            pltpu.ACC(0)((near_table.shape[0], 2 * width), jnp.float32),
+            pltpu.ACC(0)((16, 2 * width), jnp.float32),
+            pltpu.ACC(1)((16, 2 * width), jnp.float32),
+        )
+        remainder = partial - pl.run_scoped(
+            functools.partial(diagonal, number),
+            pltpu.ACC(0)((16, 2 * width), jnp.float32),
+            pltpu.ACC(1)((16, 2 * width), jnp.float32),
+        )
         following = a * v + b * remainder
 
         @pl.when(number < DEG)

time: 42.3 us -> 42.1 us (level)
  no operation moved by 1% of the time
where the time goes in v6:
time: 42.1 us; the launch traced here: 42 us
  Pallas kernels  41.4 us (98%)
  between operations  0.64 us (2%)
    pallas_call x1, Pallas kernels, local(): pl.pallas_call(functools.partial(kernel, sizes), out_shape=pltpu.VMEM((2,...  40.8 us

profile of v6, /device:TPU:1, one launch (start us, length us, event | category | flops | bytes accessed | tf_op | source)
XLA Modules:
  0.0 42.0 jit_solution(4045349278328666837)
XLA Ops:
  0.6 40.8 %shard_map.68.both_ref = f32[2,2,1,2,128]{4,3,2,1,0:T(2,128)S(1)} custom-call(bf16[108,128,128]{2,1,0:T(8,128)(2,1)} %bitcast.1, s32[2,1,8]{2,1,0:T(1,128)} %order_hbm.1, s32[2,1,8,27]{3,2,1,0:T(8,128)} %pattern_hbm.1, f32[2,1,2,128]{3,2,1,0:T(2,128)} %start_hbm.1, f32[2,1,2,128]{3,2,1,0:T(2,128)} %rhs_hbm.1), custom_call_target="tpu_custom_call" | custom-call | tf_op jit(solution)/shard_map/pallas_call | solution.py:309
  41.4 0.6 %shard_map.69 = (f32[2,1,2,128]{3,2,1,0:T(2,128)}, f32[2,1,2,128]{3,2,1,0:T(2,128)}) custom-call(f32[2,2,1,2,128]{4,3,2,1,0:T(2,128)S(1)} %shard_map.68.both_ref), custom_call_target="tpu_custom_call" | custom-call | tf_op jit(solution)/shard_map/pallas_call | solution.py:342

commit v7 on v6

--- a/solution.py
+++ b/solution.py
@@ -215,16 +215,15 @@
                 pltpu.matmul_acc_lhs(acc, left, n % 2)
         return own_rows([pltpu.matmul_pop(acc)[0:8] for acc, _ in units])
 
-    def diagonal_row(r, j):
-        last = far_rows.shape[0] - 1
-        part = jnp.broadcast_to(far_rows[pl.ds(jnp.clip(spot_of[r, j], 0, last), 1), :], (8, width))
+    def diagonal_row(spots_now, r, j):
+        part = jnp.broadcast_to(far_rows[pl.ds(spots_now[r][j], 1), :], (8, width))
         for s in range(1, depth):
-            line = jnp.broadcast_to(far_rows[pl.ds(jnp.clip(spot_of[r + s, j], 0, last), 1), :], (8, width))
+            line = jnp.broadcast_to(far_rows[pl.ds(spots_now[r + s][j], 1), :], (8, width))
             part = jnp.where(own == r + s, line, part)
         return part
 
-    def diagonal_left(r, first):
-        left = jnp.concatenate([diagonal_row(r, first), diagonal_row(r, first + 1)], axis=1)
+    def diagonal_left(spots_now, r, first):
+        left = jnp.concatenate([diagonal_row(spots_now, r, first), diagonal_row(spots_now, r, first + 1)], axis=1)
         return jnp.concatenate([left, jnp.zeros_like(left)], axis=0).astype(jnp.bfloat16)
 
     def diagonal(number, unit_0, unit_1):
@@ -232,15 +231,17 @@
         for i, (_, r) in enumerate(units):
             pltpu.matmul_push_rhs(weights(FAR_ENTRIES, r, 0), 0, i)
             pltpu.matmul_push_rhs(weights(FAR_ENTRIES, r, 2), 1, i)
+        last = far_rows.shape[0] - 1
+        spots_now = [[jnp.clip(spot_of[r, j], 0, last) for j in range(len(FAR_ENTRIES))] for r in range(rows)]
         theirs = far.at[number]
         pltpu.make_async_copy(theirs, theirs, far_sem.at[number]).wait()
         far_rows[pl.ds(8, 4 * rows * len(FAR)), :] = far[number].astype(jnp.float32)
         for i, (acc, r) in enumerate(units):
-            pltpu.matmul_acc_lhs(acc, diagonal_left(r, 0), 0)
+            pltpu.matmul_acc_lhs(acc, diagonal_left(spots_now, r, 0), 0)
             pltpu.matmul_push_rhs(weights(FAR_ENTRIES, r, 4), 0, i)
         for i, (acc, r) in enumerate(units):
-            pltpu.matmul_acc_lhs(acc, diagonal_left(r, 2), 1)
-            pltpu.matmul_acc_lhs(acc, diagonal_left(r, 4), 0)
+            pltpu.matmul_acc_lhs(acc, diagonal_left(spots_now, r, 2), 1)
+            pltpu.matmul_acc_lhs(acc, diagonal_left(spots_now, r, 4), 0)
         return own_rows([pltpu.matmul_pop(acc)[0:8] for acc, _ in units])
 
     def turn_of(number, carry):

time: 42.1 us -> 42.1 us (level)
  no operation moved by 1% of the time
where the time goes in v7:
time: 42.1 us; the launch traced here: 42 us
  Pallas kernels  41.4 us (98%)
  between operations  0.64 us (2%)
    pallas_call x1, Pallas kernels, local(): pl.pallas_call(functools.partial(kernel, sizes), out_shape=pltpu.VMEM((2,...  40.8 us

profile of v7, /device:TPU:1, one launch (start us, length us, event | category | flops | bytes accessed | tf_op | source)
XLA Modules:
  0.0 42.0 jit_solution(16960862173856010039)
XLA Ops:
  0.6 40.8 %shard_map.68.both_ref = f32[2,2,1,2,128]{4,3,2,1,0:T(2,128)S(1)} custom-call(bf16[108,128,128]{2,1,0:T(8,128)(2,1)} %bitcast.1, s32[2,1,8]{2,1,0:T(1,128)} %order_hbm.1, s32[2,1,8,27]{3,2,1,0:T(8,128)} %pattern_hbm.1, f32[2,1,2,128]{3,2,1,0:T(2,128)} %start_hbm.1, f32[2,1,2,128]{3,2,1,0:T(2,128)} %rhs_hbm.1), custom_call_target="tpu_custom_call" | custom-call | tf_op jit(solution)/shard_map/pallas_call | solution.py:310
  41.4 0.6 %shard_map.69 = (f32[2,1,2,128]{3,2,1,0:T(2,128)}, f32[2,1,2,128]{3,2,1,0:T(2,128)}) custom-call(f32[2,2,1,2,128]{4,3,2,1,0:T(2,128)S(1)} %shard_map.68.both_ref), custom_call_target="tpu_custom_call" | custom-call | tf_op jit(solution)/shard_map/pallas_call | solution.py:343

commit v8 on v7

--- a/solution.py
+++ b/solution.py
@@ -10,11 +10,13 @@
 DEG = 4
 MESH = pl.DeviceIdType.MESH
 
-NEAR = ((-1, 0), (1, 0), (0, -1), (0, 1), (0, 0))
+CORE = ((0, 0),)
+NEAR = ((-1, 0), (1, 0), (0, -1), (0, 1))
 FAR = ((1, 1), (-1, -1), (1, -1), (-1, 1))
 TURNS = (1, 2, 3, 0)
 ISSUE = (2, 1, 3, 0)
-NEAR_ENTRIES = [(9 * a + 3 * b + c, 9 * d + 3 * b + c) for a, d in ((1, 1), (2, 0)) for b in range(3) for c in range(3)]
+CORE_ENTRIES = [(9 * a + 3 + c, 9 * d + 3 + c) for a, d in ((1, 1), (2, 0)) for c in range(3)]
+NEAR_ENTRIES = [(9 * a + 3 * b + c, 9 * d + 3 * b + c) for a, d in ((1, 1), (2, 0)) for b in (0, 2) for c in range(3)]
 NEAR_ENTRIES += [(3 + c, 21 + c) for c in range(3)]
 FAR_ENTRIES = [(3 * b + c, 18 + 3 * b + c) for b in (0, 2) for c in range(3)]
 
@@ -33,20 +35,20 @@
 
 
 def kernel(sizes, blocks_hbm, order_hbm, pattern_hbm, start_hbm, rhs_hbm, out_ref,
-           blocks, turned, order_ref, pattern, first, rhs, near, far, sent, tags, tag_out, near_table, masks, far_rows, spots, spot_of,
-           load_sem, send_sem, near_sem, far_sem, tag_send, tag_recv):
+           blocks, turned, order_ref, pattern, first, rhs, core, near, far, sent, tags, tag_out, core_table, near_table, masks, far_rows, spots, spot_of,
+           load_sem, send_sem, core_sem, near_sem, far_sem, tag_send, tag_recv):
     nx, ny, nz = sizes
     gx, gy, gz = (lax.axis_index(a) for a in ("gx", "gy", "gz"))
     wide, _, depth, width = first.shape
     rows = wide * depth
-    near_peers, far_peers = 4 * len(NEAR) - 1, 4 * len(FAR)
+    core_peers, near_peers, far_peers = 4 * len(CORE) - 1, 4 * len(NEAR), 4 * len(FAR)
 
     def at(dx, dy, dz):
         return (lax.rem(gx + (dx + nx), nx), lax.rem(gy + (dy + ny), ny), lax.rem(gz + dz, nz))
 
     barrier = pltpu.get_barrier_semaphore()
     for dz in ISSUE:
-        for dx, dy in FAR + NEAR:
+        for dx, dy in FAR + NEAR + CORE:
             if (dx, dy, dz) != (0, 0, 0):
                 pl.semaphore_signal(barrier, inc=1, device_id=at(dx, dy, dz), device_id_type=MESH)
 
@@ -113,11 +115,12 @@
 
     premask(NEAR_ENTRIES, NEAR, 0)
     premask(FAR_ENTRIES, FAR, len(NEAR_ENTRIES))
-
-    pl.semaphore_wait(barrier, near_peers + far_peers)
+    premask(CORE_ENTRIES, CORE, len(NEAR_ENTRIES + FAR_ENTRIES))
+
+    pl.semaphore_wait(barrier, core_peers + near_peers + far_peers)
 
     def send(number):
-        for groups, buffer, sem in ((FAR, far, far_sem), (NEAR, near, near_sem)):
+        for groups, buffer, sem in ((FAR, far, far_sem), (NEAR, near, near_sem), (CORE, core, core_sem)):
             for dz in ISSUE:
                 for g, (dx, dy) in enumerate(groups):
                     if (dx, dy, dz) == (0, 0, 0):
@@ -128,7 +131,7 @@
                         sem.at[number], device_id=at(dx, dy, dz), device_id_type=MESH,
                     ).start()
 
-    everyone = FAR + NEAR
+    everyone = FAR + NEAR + CORE
     for g, (dx, dy) in enumerate(everyone[:-1]):
         pltpu.make_async_remote_copy(
             tag_out, tags.at[g], tag_send, tag_recv, device_id=at(dx, dy, 0), device_id_type=MESH
@@ -163,6 +166,7 @@
             both = jnp.concatenate(parts[j : j + 2], axis=0)
             table[pl.ds(8 * j, 16), :] = both.astype(jnp.bfloat16)
 
+    finish(CORE_ENTRIES, len(NEAR_ENTRIES + FAR_ENTRIES), len(FAR + NEAR), len(CORE), core_table)
     finish(NEAR_ENTRIES, 0, len(FAR), len(NEAR), near_table)
     plane = jnp.zeros((8, width), jnp.float32)
     for g in range(len(FAR)):
@@ -195,24 +199,27 @@
                 product = jnp.where(own == r + s, total[:, s * width : (s + 1) * width], product)
         return product
 
-    def nearby(number, picked_0, unit_0, unit_1):
-        seen = near[number]
+    def nearby(entries, table_ref, theirs, sem, group, picked_0, unit_0, unit_1):
+        units = list(zip((unit_0, unit_1), range(0, rows, depth)))
+        pltpu.matmul_push_rhs(weights(entries, units[1][1], 0), 0, 1)
+        pltpu.matmul_push_rhs(weights(entries, units[1][1], 2), 1, 1)
+        pltpu.matmul_push_rhs(weights(entries, units[0][1], 0), 1, 0)
+        pltpu.make_async_copy(theirs, theirs, sem).wait()
+        seen = group[...]
         seen = jnp.concatenate([seen, jnp.zeros((2 * width - seen.shape[0], width), jnp.bfloat16)], axis=0)
         pltpu.matmul_push_rhs(jnp.concatenate([seen, jnp.zeros_like(seen)], axis=1), 0, 0)
-        units = list(zip((unit_0, unit_1), range(0, rows, depth)))
-        pltpu.matmul_push_rhs(weights(NEAR_ENTRIES, units[1][1], 0), 0, 1)
-        table = near_table[...]
+        table = table_ref[...]
         pltpu.matmul_acc_lhs(picked_0, jnp.concatenate([table, jnp.zeros_like(table)], axis=1), 0)
-        pltpu.matmul_push_rhs(weights(NEAR_ENTRIES, units[0][1], 0), 0, 0)
+        pltpu.matmul_push_rhs(weights(entries, units[0][1], 2), 0, 0)
         picked = pltpu.matmul_pop(picked_0)[:, 0:width]
-        chunks = range(0, len(NEAR_ENTRIES), 2)
-        for n, first in enumerate(chunks):
+        for n, first in enumerate(range(0, len(entries), 2)):
             left = jnp.concatenate([picked[8 * first : 8 * first + 8], picked[8 * first + 8 : 8 * first + 16]], axis=1)
             left = jnp.concatenate([left, jnp.zeros_like(left)], axis=0).astype(jnp.bfloat16)
             for i, (acc, r) in enumerate(units):
-                if n + 1 < len(chunks):
-                    pltpu.matmul_push_rhs(weights(NEAR_ENTRIES, r, first + 2), (n + 1) % 2, i)
-                pltpu.matmul_acc_lhs(acc, left, n % 2)
+                staged = (n + 1 - i) % 2
+                pltpu.matmul_acc_lhs(acc, left, staged)
+                if first + 4 < len(entries):
+                    pltpu.matmul_push_rhs(weights(entries, r, first + 4), staged, i)
         return own_rows([pltpu.matmul_pop(acc)[0:8] for acc, _ in units])
 
     def diagonal_row(spots_now, r, j):
@@ -228,20 +235,19 @@
 
     def diagonal(number, unit_0, unit_1):
         units = list(zip((unit_0, unit_1), range(0, rows, depth)))
-        for i, (_, r) in enumerate(units):
+        for i, (acc, r) in enumerate(units):
             pltpu.matmul_push_rhs(weights(FAR_ENTRIES, r, 0), 0, i)
-            pltpu.matmul_push_rhs(weights(FAR_ENTRIES, r, 2), 1, i)
+            pltpu.matmul_acc_lhs(acc, jnp.zeros((16, 2 * width), jnp.bfloat16), 0)
+            pltpu.matmul_push_rhs(weights(FAR_ENTRIES, r, 2), 0, i)
+            pltpu.matmul_push_rhs(weights(FAR_ENTRIES, r, 4), 1, i)
         last = far_rows.shape[0] - 1
         spots_now = [[jnp.clip(spot_of[r, j], 0, last) for j in range(len(FAR_ENTRIES))] for r in range(rows)]
         theirs = far.at[number]
         pltpu.make_async_copy(theirs, theirs, far_sem.at[number]).wait()
         far_rows[pl.ds(8, 4 * rows * len(FAR)), :] = far[number].astype(jnp.float32)
-        for i, (acc, r) in enumerate(units):
-            pltpu.matmul_acc_lhs(acc, diagonal_left(spots_now, r, 0), 0)
-            pltpu.matmul_push_rhs(weights(FAR_ENTRIES, r, 4), 0, i)
-        for i, (acc, r) in enumerate(units):
-            pltpu.matmul_acc_lhs(acc, diagonal_left(spots_now, r, 2), 1)
-            pltpu.matmul_acc_lhs(acc, diagonal_left(spots_now, r, 4), 0)
+        for first, staged in ((0, None), (2, 0), (4, 1)):
+            for acc, r in units:
+                pltpu.matmul_acc_lhs(acc, diagonal_left(spots_now, r, first), staged)
         return own_rows([pltpu.matmul_pop(acc)[0:8] for acc, _ in units])
 
     def turn_of(number, carry):
@@ -250,15 +256,18 @@
         for i in range(1, DEG):
             a = jnp.where(number == i, jnp.float32(old[i]), a)
             b = jnp.where(number == i, jnp.float32(new[i]), b)
-        near[number, pl.ds(near_peers * rows, rows)] = sent[number]
-        theirs = near.at[number, pl.ds(0, near_peers * rows)]
-        pltpu.make_async_copy(theirs, theirs, near_sem.at[number]).wait()
-        partial = remainder - pl.run_scoped(
-            functools.partial(nearby, number),
-            pltpu.ACC(0)((near_table.shape[0], 2 * width), jnp.float32),
-            pltpu.ACC(0)((16, 2 * width), jnp.float32),
-            pltpu.ACC(1)((16, 2 * width), jnp.float32),
-        )
+        core[number, pl.ds(core_peers * rows, rows)] = sent[number]
+        def applied(entries, table, theirs, sem, group):
+            return pl.run_scoped(
+                functools.partial(nearby, entries, table, theirs, sem, group),
+                pltpu.ACC(0)((table.shape[0], 2 * width), jnp.float32),
+                pltpu.ACC(0)((16, 2 * width), jnp.float32),
+                pltpu.ACC(1)((16, 2 * width), jnp.float32),
+            )
+
+        mates = core.at[number, pl.ds(0, core_peers * rows)]
+        partial = remainder - applied(CORE_ENTRIES, core_table, mates, core_sem.at[number], core.at[number])
+        partial = partial - applied(NEAR_ENTRIES, near_table, near.at[number], near_sem.at[number], near.at[number])
         remainder = partial - pl.run_scoped(
             functools.partial(diagonal, number),
             pltpu.ACC(0)((16, 2 * width), jnp.float32),
@@ -281,10 +290,8 @@
     pltpu.make_async_copy(others, others, tag_send).wait()
 
     def drain(number, carry):
-        theirs = near.at[number, pl.ds(0, near_peers * rows)]
-        pltpu.make_async_copy(theirs, theirs, send_sem.at[number]).wait()
-        theirs = far.at[number]
-        pltpu.make_async_copy(theirs, theirs, send_sem.at[number]).wait()
+        for theirs in (core.at[number, pl.ds(0, core_peers * rows)], near.at[number], far.at[number]):
+            pltpu.make_async_copy(theirs, theirs, send_sem.at[number]).wait()
         return carry
 
     lax.fori_loop(0, DEG + 1, drain, 0)
@@ -306,7 +313,7 @@
     flat = blocks.reshape((rows * blocks.shape[3],) + blocks.shape[4:])
     vmem = pl.BlockSpec(memory_space=pltpu.VMEM)
     anywhere = pl.BlockSpec(memory_space=pl.ANY)
-    near_blocks = (len(NEAR_ENTRIES) + 1) // 2
+    core_blocks, near_blocks = (len(CORE_ENTRIES) + 1) // 2, (len(NEAR_ENTRIES) + 1) // 2
     both = pl.pallas_call(
         functools.partial(kernel, sizes),
         out_shape=pltpu.VMEM((2,) + start.shape, jnp.float32),
@@ -319,17 +326,20 @@
             pltpu.VMEM(pattern.shape, jnp.int32),
             pltpu.VMEM(start.shape, jnp.float32),
             pltpu.VMEM(start.shape, jnp.float32),
+            pltpu.VMEM((DEG + 1, 4 * rows * len(CORE), width), jnp.bfloat16),
             pltpu.VMEM((DEG + 1, 4 * rows * len(NEAR), width), jnp.bfloat16),
             pltpu.VMEM((DEG + 1, 4 * rows * len(FAR), width), jnp.bfloat16),
             pltpu.VMEM((DEG + 1, rows, width), jnp.bfloat16),
-            pltpu.VMEM((len(NEAR) + len(FAR), 8, width), jnp.float32),
+            pltpu.VMEM((len(CORE + NEAR + FAR), 8, width), jnp.float32),
             pltpu.VMEM((8, width), jnp.float32),
+            pltpu.VMEM((16 * core_blocks, width), jnp.bfloat16),
             pltpu.VMEM((16 * near_blocks, width), jnp.bfloat16),
-            pltpu.VMEM((len(NEAR_ENTRIES) + len(FAR_ENTRIES), 8, width), jnp.float32),
+            pltpu.VMEM((len(NEAR_ENTRIES + FAR_ENTRIES + CORE_ENTRIES), 8, width), jnp.float32),
             pltpu.VMEM((8 + 4 * rows * len(FAR), width), jnp.float32),
             pltpu.VMEM((8, width), jnp.int32),
             pltpu.SMEM((8, width), jnp.int32),
             pltpu.SemaphoreType.DMA((5,)),
+            pltpu.SemaphoreType.DMA((DEG + 1,)),
             pltpu.SemaphoreType.DMA((DEG + 1,)),
             pltpu.SemaphoreType.DMA((DEG + 1,)),
             pltpu.SemaphoreType.DMA((DEG + 1,)),

time: 42.1 us -> 42.3 us (level)
  no operation moved by 1% of the time
where the time goes in v8:
time: 42.3 us; the launch traced here: 42.2 us
  Pallas kernels  41.6 us (98%)
  between operations  0.64 us (2%)
    pallas_call x1, Pallas kernels, local(): pl.pallas_call(functools.partial(kernel, sizes), out_shape=pltpu.VMEM((2,...  41 us

profile of v8, /device:TPU:1, one launch (start us, length us, event | category | flops | bytes accessed | tf_op | source)
XLA Modules:
  0.0 42.2 jit_solution(8741123473229645690)
XLA Ops:
  0.6 41.0 %shard_map.68.both_ref = f32[2,2,1,2,128]{4,3,2,1,0:T(2,128)S(1)} custom-call(bf16[108,128,128]{2,1,0:T(8,128)(2,1)} %bitcast.1, s32[2,1,8]{2,1,0:T(1,128)} %order_hbm.1, s32[2,1,8,27]{3,2,1,0:T(8,128)} %pattern_hbm.1, f32[2,1,2,128]{3,2,1,0:T(2,128)} %start_hbm.1, f32[2,1,2,128]{3,2,1,0:T(2,128)} %rhs_hbm.1), custom_call_target="tpu_custom_call" | custom-call | tf_op jit(solution)/shard_map/pallas_call | solution.py:317
  41.6 0.6 %shard_map.69 = (f32[2,1,2,128]{3,2,1,0:T(2,128)}, f32[2,1,2,128]{3,2,1,0:T(2,128)}) custom-call(f32[2,2,1,2,128]{4,3,2,1,0:T(2,128)S(1)} %shard_map.68.both_ref), custom_call_target="tpu_custom_call" | custom-call | tf_op jit(solution)/shard_map/pallas_call | solution.py:353
